TPU v7x, 32 devices: a whole 2x2x4 slice. The times are simulated.
32 devices in a mesh: groups: 2 (over y), seq: 4 (over z), tensor: 4 (over x, core).
Axes of the slice: x: 2, y: 2, z: 4, core: 2. Of those that a mesh axis runs over, the one named last changes fastest.
Arguments:
- queries: bfloat16 [2048, 4096], P(('groups', 'seq'), 'tensor'), parts along dimension 0, may hold values from -6 to 6
- key_rows: bfloat16 [2048, 2048], P(('groups', 'seq'), 'tensor'), parts along dimension 0, may hold values from -6 to 6
- value_rows: bfloat16 [2048, 2048], P(('groups', 'seq'), 'tensor'), parts along dimension 0, may hold values from -6 to 6
- positions: int32 [2048], P(('groups', 'seq')), parts along dimension 0, may hold values from 0 to 131071, as said below
- residual: bfloat16 [2048, 3840], P(('groups', 'seq'), 'tensor'), parts along dimension 0, may hold values from -16 to 16
- direction: float32 [7680], P('groups'), parts along dimension 0, may hold values from -90 to 90
- out_weight: bfloat16 [4096, 3840], P('tensor'), may hold values from -0.375 to 0.375
Outputs:
- ablated: bfloat16 [2048, 3840], P(('groups', 'seq'), 'tensor'), parts along dimension 0
There are 2 independent parts, one for each index of `groups`. A program takes and returns all parts, laid end to end along the dimension named above; an argument that names none is the same for every part. Nothing has to cross between parts.
Inputs may be any that keep to these rules, and one draw needn't show every extreme that they name: positions strictly increase along the slab, by at most 4 from one token to the next; the slab ends at the prompt's last position.
All inputs are finite; a program needn't handle non-finite values.
Results may differ from a plain program's by a relative error of at most 0.017.
Values may be sent and summed in bfloat16 or wider, within the bound.
No kernel may reach another device: no remote copies, remote signals or barrier semaphores. Data moves between devices by JAX's collectives and lax.ppermute only.
A program may use at most 64 MiB of HBM per device.

v0:
```python
import jax
import jax.numpy as jnp
from jax import lax
from jax.sharding import PartitionSpec as P

HD = 256
WINDOW = 1024


big_negative = -1e30


def shifted_2(value, axis, steps):
    count = lax.axis_size(axis)
    first, last = (max(0, -steps), min(count, count - steps))
    return lax.ppermute(value, axis, [(source, source + steps) for source in range(first, last)])


def rotary_tables(positions, head_dim):
    half_dim = head_dim // 2
    freqs = jnp.power(10000.0, -jnp.arange(half_dim, dtype=jnp.float32) * 2.0 / head_dim)
    angles = positions.astype(jnp.float32)[:, None] * freqs[None, :]
    return (jnp.cos(angles)[:, None, :], jnp.sin(angles)[:, None, :])


def rotate_heads(block, cos_table, sin_table, head_dim):
    row_count = block.shape[0]
    head_count = block.shape[1] // head_dim
    half_dim = head_dim // 2
    widened = block.reshape(row_count, head_count, head_dim).astype(jnp.float32)
    first_half = widened[:, :, :half_dim]
    second_half = widened[:, :, half_dim:]
    turned = jnp.concatenate(
        [
            first_half * cos_table - second_half * sin_table,
            second_half * cos_table + first_half * sin_table,
        ],
        axis=-1,
    )
    return turned.reshape(row_count, head_count * head_dim)


def body(queries, key_rows, value_rows, positions, residual, direction, out_weight):
    tokens_here = queries.shape[0]
    query_heads = queries.shape[1] // HD
    kv_heads = key_rows.shape[1] // HD
    group_size = query_heads // kv_heads
    span_blocks = WINDOW // tokens_here
    seq_index = lax.axis_index("seq")
    cos_table, sin_table = rotary_tables(positions, HD)
    rot_queries = (rotate_heads(queries, cos_table, sin_table, HD) * HD ** (-0.5)).astype(
        jnp.bfloat16
    )
    rot_keys = rotate_heads(key_rows, cos_table, sin_table, HD).astype(jnp.bfloat16)
    query_blocks = rot_queries.reshape(tokens_here, kv_heads, group_size, HD)
    own_scores = jnp.einsum(
        "qkgd,skd->kgqs",
        query_blocks,
        rot_keys.reshape(tokens_here, kv_heads, HD),
        preferred_element_type=jnp.float32,
    )
    earlier_keys = []
    earlier_values = []
    for distance in range(span_blocks, 0, -1):
        moved_keys, moved_values = shifted_2((rot_keys, value_rows), "seq", distance)
        earlier_keys.append(moved_keys)
        earlier_values.append(moved_values)
    far_keys = jnp.concatenate(earlier_keys, axis=0)
    far_values = jnp.concatenate(earlier_values, axis=0)
    far_scores = jnp.einsum(
        "qkgd,skd->kgqs",
        query_blocks,
        far_keys.reshape(-1, kv_heads, HD),
        preferred_element_type=jnp.float32,
    )
    scores = jnp.concatenate([far_scores, own_scores], axis=-1)
    query_index = seq_index * tokens_here + jnp.arange(tokens_here, dtype=jnp.int32)
    key_index = (seq_index - span_blocks) * tokens_here + jnp.arange(
        (span_blocks + 1) * tokens_here, dtype=jnp.int32
    )
    gap_grid = query_index[:, None] - key_index[None, :]
    allowed = (gap_grid >= 0) & (gap_grid < WINDOW) & (key_index[None, :] >= 0)
    scores = jnp.where(allowed, scores, big_negative)
    row_max = jnp.max(scores, axis=-1, keepdims=True)
    shifted = jnp.exp(scores - row_max)
    row_sum = jnp.sum(shifted, axis=-1, keepdims=True)
    weights = (shifted / row_sum).astype(jnp.bfloat16)
    every_value = jnp.concatenate([far_values, value_rows], axis=0).reshape(-1, kv_heads, HD)
    mixed = jnp.einsum("kgqs,skd->qkgd", weights, every_value, preferred_element_type=jnp.float32)
    attended = mixed.astype(jnp.bfloat16).reshape(tokens_here, query_heads * HD)
    partial_value = jnp.dot(attended, out_weight, preferred_element_type=jnp.float32)
    unit_dir = direction / jnp.sqrt(jnp.sum(direction * direction) + 1e-06)
    column_width = residual.shape[1]
    tensor_index = lax.axis_index("tensor")
    local_dir = lax.dynamic_slice_in_dim(unit_dir, tensor_index * column_width, column_width, 0)
    base_state = residual.astype(jnp.float32)
    rounded_terms = partial_value.astype(jnp.bfloat16).astype(jnp.float32)
    dot_terms = jnp.sum(rounded_terms * unit_dir[None, :], axis=1) + jnp.sum(
        base_state * local_dir[None, :], axis=1
    )
    along = lax.psum(dot_terms, "tensor")
    summed = lax.psum_scatter(
        partial_value.astype(jnp.bfloat16), "tensor", scatter_dimension=1, tiled=True
    ).astype(jnp.float32)
    hidden_state = base_state + summed
    ablated = (hidden_state - along[:, None] * local_dir[None, :]).astype(jnp.bfloat16)
    return ablated


def solution(mesh):
    return jax.shard_map(
        body,
        mesh=mesh,
        in_specs=(
            P(("groups", "seq"), "tensor"),
            P(("groups", "seq"), "tensor"),
            P(("groups", "seq"), "tensor"),
            P(("groups", "seq")),
            P(("groups", "seq"), "tensor"),
            P("groups"),
            P("tensor", None),
        ),
        out_specs=P(("groups", "seq"), "tensor"),
        check_vma=False,
    )
```

profile of v0, /device:TPU:0, one launch (start us, length us, event | category | flops | bytes accessed | tf_op | source)
XLA Modules:
  0.0 118.3 jit_solution(2316174666957197548)
XLA Ops:
  6.5 0.8 collective-permute-start
  7.3 7.0 %collective-permute-start.1 = (bf16[256,512]{1,0:T(8,128)(2,1)}, bf16[256,512]{1,0:T(8,128)(2,1)S(1)}, u32[]{:S(2)}, u32[]{:S(2)}) collective-permute-start(bf16[256,512]{1,0:T(8,128)(2,1)} %param.9), channel_id=1, source_target_pairs={{0,12},{1,13},{2,14},{3,15},{16,28},{17,29},{18,30},{19,31}} | collective-permute-start | bytes 786440 | tf_op jit(solution)/shard_map/ppermute | solution.py:16
  14.3 1.3 %collective-permute-start.2 = (bf16[256,512]{1,0:T(8,128)(2,1)}, bf16[256,512]{1,0:T(8,128)(2,1)S(1)}, u32[]{:S(2)}, u32[]{:S(2)}) collective-permute-start(bf16[256,512]{1,0:T(8,128)(2,1)} %param.9), channel_id=1, source_target_pairs={{0,8},{4,12},{1,9},{5,13},{2,10},{6,14},{3,11},{7,15},{16,24},{20,... | collective-permute-start | bytes 786440 | tf_op jit(solution)/shard_map/ppermute | solution.py:16
  15.7 2.5 %collective-permute-start.3 = (bf16[256,512]{1,0:T(8,128)(2,1)}, bf16[256,512]{1,0:T(8,128)(2,1)S(1)}, u32[]{:S(2)}, u32[]{:S(2)}) collective-permute-start(bf16[256,512]{1,0:T(8,128)(2,1)} %param.9), channel_id=1, source_target_pairs={{0,4},{4,8},{8,12},{1,5},{5,9},{9,13},{2,6},{6,10},{10,14},{3,7},{... | collective-permute-start | bytes 786440 | tf_op jit(solution)/shard_map/ppermute | solution.py:16
  18.8 1.1 copy.37
  20.9 0.8 copy.40
  21.7 2.6 %collective-permute-start.7 = (bf16[256,512]{0,1:T(8,128)(2,1)}, bf16[256,512]{0,1:T(8,128)(2,1)}, u32[]{:S(2)}, u32[]{:S(2)}) collective-permute-start(bf16[256,512]{0,1:T(8,128)(2,1)} %bitcast.5), channel_id=1, source_target_pairs={{0,4},{4,8},{8,12},{1,5},{5,9},{9,13},{2,6},{6,10},{10,14},{3,7},{... | collective-permute-start | bytes 786440 | tf_op jit(solution)/shard_map/ppermute | solution.py:16
  25.2 1.3 %convolution_bitcast_fusion.1 = f32[2,2,256,256]{2,3,1,0:T(8,128)} fusion(bf16[256,2,2,256]{3,0,2,1:T(8,128)(2,1)S(1)} %bitcast.36, bf16[256,2,128]{2,0,1:T(8,128)(2,1)S(1)} %get-tuple-element.10, bf16[256,2,128]{2,0,1:T(8,128)(2,1)S(1)} %get-tuple-element.9), kind=kOutput, calls=%fused_computation.14 | convolution fusion | flops 134742016 | bytes 1835008 | tf_op jit(solution)/shard_map/qkgd,skd->kgqs/dot_general | solution.py:56
  26.5 0.9 fusion.7
  28.8 2.0 %collective-permute-start.6 = (bf16[256,512]{0,1:T(8,128)(2,1)}, bf16[256,512]{0,1:T(8,128)(2,1)}, u32[]{:S(2)}, u32[]{:S(2)}) collective-permute-start(bf16[256,512]{0,1:T(8,128)(2,1)} %bitcast.5), channel_id=1, source_target_pairs={{0,8},{4,12},{1,9},{5,13},{2,10},{6,14},{3,11},{7,15},{16,24},{20,... | collective-permute-start | bytes 786440 | tf_op jit(solution)/shard_map/ppermute | solution.py:16
  30.9 2.0 %collective-permute-start.5 = (bf16[256,512]{0,1:T(8,128)(2,1)}, bf16[256,512]{0,1:T(8,128)(2,1)}, u32[]{:S(2)}, u32[]{:S(2)}) collective-permute-start(bf16[256,512]{0,1:T(8,128)(2,1)} %bitcast.5), channel_id=1, source_target_pairs={{0,12},{1,13},{2,14},{3,15},{16,28},{17,29},{18,30},{19,31}} | collective-permute-start | bytes 786440 | tf_op jit(solution)/shard_map/ppermute | solution.py:16
  32.9 1.4 %collective-permute-start.4 = (bf16[256,512]{0,1:T(8,128)(2,1)}, bf16[256,512]{0,1:T(8,128)(2,1)}, u32[]{:S(2)}, u32[]{:S(2)}) collective-permute-start(bf16[256,512]{0,1:T(8,128)(2,1)} %bitcast.5), channel_id=1, source_target_pairs={} | collective-permute-start | bytes 786440 | tf_op jit(solution)/shard_map/ppermute | solution.py:16
  35.0 3.3 %collective-permute-done.7 = bf16[256,512]{0,1:T(8,128)(2,1)} collective-permute-done((bf16[256,512]{0,1:T(8,128)(2,1)}, bf16[256,512]{0,1:T(8,128)(2,1)}, u32[]{:S(2)}, u32[]{:S(2)}) %collective-permute-start.7) | collective-permute-done | bytes 262176 | tf_op jit(solution)/shard_map/ppermute | solution.py:16
  38.3 5.7 %collective-permute-done.6 = bf16[256,512]{0,1:T(8,128)(2,1)} collective-permute-done((bf16[256,512]{0,1:T(8,128)(2,1)}, bf16[256,512]{0,1:T(8,128)(2,1)}, u32[]{:S(2)}, u32[]{:S(2)}) %collective-permute-start.6) | collective-permute-done | bytes 262176 | tf_op jit(solution)/shard_map/ppermute | solution.py:16
  43.9 4.5 %collective-permute-done.5 = bf16[256,512]{0,1:T(8,128)(2,1)} collective-permute-done((bf16[256,512]{0,1:T(8,128)(2,1)}, bf16[256,512]{0,1:T(8,128)(2,1)}, u32[]{:S(2)}, u32[]{:S(2)}) %collective-permute-start.5) | collective-permute-done | bytes 262176 | tf_op jit(solution)/shard_map/ppermute | solution.py:16
  48.4 1.3 %pad_maximum_fusion = bf16[1024,512]{0,1:T(8,128)(2,1)S(1)} fusion(bf16[256,512]{0,1:T(8,128)(2,1)} %collective-permute-done.7, bf16[256,512]{0,1:T(8,128)(2,1)} %collective-permute-done.6, bf16[256,512]{0,1:T(8,128)(2,1)} %collective-permute-done.5, bf16[256,512]{0,1:T(8,128)(2,1)} %collective-permute-done.4), kind=kLoop, calls=%fused_computation.20 | loop fusion | flops 4194304 | bytes 2097152 | tf_op jit(solution)/shard_map/concatenate | solution.py:68
  49.8 0.9 convolution_bitcast_fusion
  51.0 1.6 %exponential_reduce_fusion = f32[2,2,256]{2,1,0:T(2,128)S(1)} fusion(f32[2,2,256,256]{2,3,1,0:T(8,128)S(1)} %copy-done.2, f32[2,2,256,1024]{2,3,1,0:T(8,128)S(1)} %convolution_bitcast_fusion, pred[256,1280]{0,1:T(8,128)(4,1)S(1)} %fusion.7), kind=kOutput, calls=%fused_computation.5 | output fusion | flops 5244159 | bytes 5574656 | tf_op jit(solution)/shard_map/sub | solution.py:85
  53.0 4.8 %fusion.8 = bf16[2,256,2,256]{3,1,2,0:T(8,128)(2,1)} fusion(bf16[1280,2,256,1]{0,2,3,1:T(8,128)(2,1)S(1)} %bitcast.40, f32[2,2,256]{2,1,0:T(2,128)S(1)} %exponential_reduce_fusion, f32[2,2,256,256]{2,3,1,0:T(8,128)S(1)} %copy-done.3, f32[2,2,256,1024]{2,3,1,0:T(8,128)} %copy-done, pred[256,1280]{0,1:T(8,128)(4,1)S(1)} %fusion.7), kind=kOutput, calls=%fused_computation.17 | convolution fusion | flops 677906688 | bytes 7409664 | tf_op jit(solution)/shard_map/kgqs,skd->qkgd/dot_general | solution.py:89
  57.7 5.7 %multiply_reduce_fusion = (f32[256]{0:T(256)S(1)}, bf16[256,3840]{1,0:T(8,128)(2,1)S(1)}) fusion(f32[3840]{0:T(1024)S(1)} %broadcast_divide_fusion, bf16[256,1024]{0,1:T(8,128)(2,1)} %bitcast.41, bf16[1024,3840]{1,0:T(8,128)(2,1)} %param.13), kind=kOutput, calls=%fused_computation.7 | convolution fusion | flops 2017197824 | bytes 10371072 | tf_op jit(solution)/shard_map/dot_general | solution.py:91
  63.5 2.3 %copy.52 = bf16[256,3840]{0,1:T(8,128)(2,1)} copy(bf16[256,3840]{1,0:T(8,128)(2,1)S(1)} %get-tuple-element.16) | data formatting | bytes 3932160
  66.1 5.7 %psum.7 = f32[256]{0:T(256)S(1)} all-reduce(f32[256]{0:T(256)S(1)} %add.55), channel_id=1, replica_groups=mesh['groups'=2,'seq'=4,'tensor'=4] {'tensor'}, use_global_device_ids=true, to_apply=%region_6.7 | all-reduce | flops 256 | bytes 2048 | tf_op jit(solution)/shard_map/psum | solution.py:101
  71.9 37.6 %reduce-scatter.4.cloned.1.call-done = bf16[960,256]{1,0:T(8,128)(2,1)} async-done(((bf16[3840,256]{1,0:T(8,128)(2,1)}), bf16[960,256]{1,0:T(8,128)(2,1)}) %reduce-scatter.4.cloned.1.call-update) | async-done | bytes 491536
  109.5 2.0 %fusion.11 = bf16[256,960]{0,1:T(8,128)(2,1)} fusion(bf16[256,960]{0,1:T(8,128)(2,1)S(1)} %copy-done.1, bf16[960,256]{1,0:T(8,128)(2,1)} %reduce-scatter.4.cloned.1.call-done, f32[256]{0:T(256)S(1)} %psum.7, f32[960]{0:T(1024)S(1)} %dynamic_slice.3), kind=kLoop, calls=%fused_computation.24 | loop fusion | flops 1474560 | bytes 1479424 | tf_op jit(solution)/shard_map/convert_element_type | solution.py:106
  (47 shorter events, 4.8 us)
Async XLA Ops:
  6.5 17.8 %copy-start.4 = (bf16[256,1024]{1,0:T(8,128)(2,1)S(1)}, bf16[256,1024]{1,0:T(8,128)(2,1)}, u32[]{:S(2)}) copy-start(bf16[256,1024]{1,0:T(8,128)(2,1)} %param.7) | copy-start | bytes 1572868
  6.5 102.9 %reduce-scatter.4.cloned.1.call-start = ((), (), s32[]{:S(2)}) async-start(), calls=%async_computation.1 | async-start | bytes 2457600
  6.5 22.3 %collective-permute-start = (bf16[256,512]{1,0:T(8,128)(2,1)}, bf16[256,512]{1,0:T(8,128)(2,1)S(1)}, u32[]{:S(2)}, u32[]{:S(2)}) collective-permute-start(bf16[256,512]{1,0:T(8,128)(2,1)} %param.9), channel_id=1, source_target_pairs={} | collective-permute-start | bytes 786440 | tf_op jit(solution)/shard_map/ppermute | solution.py:16
  7.3 23.5 %collective-permute-start.1 = (bf16[256,512]{1,0:T(8,128)(2,1)}, bf16[256,512]{1,0:T(8,128)(2,1)S(1)}, u32[]{:S(2)}, u32[]{:S(2)}) collective-permute-start(bf16[256,512]{1,0:T(8,128)(2,1)} %param.9), channel_id=1, source_target_pairs={{0,12},{1,13},{2,14},{3,15},{16,28},{17,29},{18,30},{19,31}} | collective-permute-start | bytes 786440 | tf_op jit(solution)/shard_map/ppermute | solution.py:16
  14.3 18.5 %collective-permute-start.2 = (bf16[256,512]{1,0:T(8,128)(2,1)}, bf16[256,512]{1,0:T(8,128)(2,1)S(1)}, u32[]{:S(2)}, u32[]{:S(2)}) collective-permute-start(bf16[256,512]{1,0:T(8,128)(2,1)} %param.9), channel_id=1, source_target_pairs={{0,8},{4,12},{1,9},{5,13},{2,10},{6,14},{3,11},{7,15},{16,24},{20,... | collective-permute-start | bytes 786440 | tf_op jit(solution)/shard_map/ppermute | solution.py:16
  15.7 18.6 %collective-permute-start.3 = (bf16[256,512]{1,0:T(8,128)(2,1)}, bf16[256,512]{1,0:T(8,128)(2,1)S(1)}, u32[]{:S(2)}, u32[]{:S(2)}) collective-permute-start(bf16[256,512]{1,0:T(8,128)(2,1)} %param.9), channel_id=1, source_target_pairs={{0,4},{4,8},{8,12},{1,5},{5,9},{9,13},{2,6},{6,10},{10,14},{3,7},{... | collective-permute-start | bytes 786440 | tf_op jit(solution)/shard_map/ppermute | solution.py:16
  21.7 16.5 %collective-permute-start.7 = (bf16[256,512]{0,1:T(8,128)(2,1)}, bf16[256,512]{0,1:T(8,128)(2,1)}, u32[]{:S(2)}, u32[]{:S(2)}) collective-permute-start(bf16[256,512]{0,1:T(8,128)(2,1)} %bitcast.5), channel_id=1, source_target_pairs={{0,4},{4,8},{8,12},{1,5},{5,9},{9,13},{2,6},{6,10},{10,14},{3,7},{... | collective-permute-start | bytes 786440 | tf_op jit(solution)/shard_map/ppermute | solution.py:16
  25.0 2.5 %copy-start.6 = (f32[3840]{0:T(1024)S(1)}, f32[3840]{0:T(1024)}, u32[]{:S(2)}) copy-start(f32[3840]{0:T(1024)} %param.12) | copy-start | bytes 46084
  25.2 9.2 %copy-start.5 = (bf16[256,512]{1,0:T(8,128)(2,1)S(1)}, bf16[256,512]{1,0:T(8,128)(2,1)}, u32[]{:S(2)}) copy-start(bf16[256,512]{1,0:T(8,128)(2,1)} %param.9) | copy-start | bytes 786436
  28.8 15.1 %collective-permute-start.6 = (bf16[256,512]{0,1:T(8,128)(2,1)}, bf16[256,512]{0,1:T(8,128)(2,1)}, u32[]{:S(2)}, u32[]{:S(2)}) collective-permute-start(bf16[256,512]{0,1:T(8,128)(2,1)} %bitcast.5), channel_id=1, source_target_pairs={{0,8},{4,12},{1,9},{5,13},{2,10},{6,14},{3,11},{7,15},{16,24},{20,... | collective-permute-start | bytes 786440 | tf_op jit(solution)/shard_map/ppermute | solution.py:16
  30.9 17.6 %collective-permute-start.5 = (bf16[256,512]{0,1:T(8,128)(2,1)}, bf16[256,512]{0,1:T(8,128)(2,1)}, u32[]{:S(2)}, u32[]{:S(2)}) collective-permute-start(bf16[256,512]{0,1:T(8,128)(2,1)} %bitcast.5), channel_id=1, source_target_pairs={{0,12},{1,13},{2,14},{3,15},{16,28},{17,29},{18,30},{19,31}} | collective-permute-start | bytes 786440 | tf_op jit(solution)/shard_map/ppermute | solution.py:16
  32.9 15.5 %collective-permute-start.4 = (bf16[256,512]{0,1:T(8,128)(2,1)}, bf16[256,512]{0,1:T(8,128)(2,1)}, u32[]{:S(2)}, u32[]{:S(2)}) collective-permute-start(bf16[256,512]{0,1:T(8,128)(2,1)} %bitcast.5), channel_id=1, source_target_pairs={} | collective-permute-start | bytes 786440 | tf_op jit(solution)/shard_map/ppermute | solution.py:16
  49.7 1.2 %copy-start.2 = (f32[2,2,256,256]{2,3,1,0:T(8,128)S(1)}, f32[2,2,256,256]{2,3,1,0:T(8,128)}, u32[]{:S(2)}) copy-start(f32[2,2,256,256]{2,3,1,0:T(8,128)} %convolution_bitcast_fusion.1) | copy-start | bytes 3145732
  51.0 1.9 %copy-start = (f32[2,2,256,1024]{2,3,1,0:T(8,128)}, f32[2,2,256,1024]{2,3,1,0:T(8,128)S(1)}, u32[]{:S(2)}) copy-start(f32[2,2,256,1024]{2,3,1,0:T(8,128)S(1)} %convolution_bitcast_fusion) | copy-start | bytes 12582916
  51.0 2.0 %copy-start.3 = (f32[2,2,256,256]{2,3,1,0:T(8,128)S(1)}, f32[2,2,256,256]{2,3,1,0:T(8,128)}, u32[]{:S(2)}) copy-start(f32[2,2,256,256]{2,3,1,0:T(8,128)} %convolution_bitcast_fusion.1) | copy-start | bytes 3145732
  63.5 2.4 %copy-start.1 = (bf16[256,960]{0,1:T(8,128)(2,1)S(1)}, bf16[256,960]{0,1:T(8,128)(2,1)}, u32[]{:S(2)}) copy-start(bf16[256,960]{0,1:T(8,128)(2,1)} %param.11) | copy-start | bytes 1474564
Sparse Core Ops, SparseCore 0:
  65.9 43.4 reduce-scatter.3
where the time goes:
time: 119 us; the launch traced here: 118 us
  waiting for transfers between devices  51.1 us (43%)
  starting transfers between devices  19.5 us (16%)
  between operations  14.4 us (12%)
  matrix products  12.8 us (11%)
  other arithmetic  8.23 us (7%)
  local copies, waits for them, and re-layouts  6.64 us (6%)
  blocking collectives  5.74 us (5%)
    unnamed x2, waiting for transfers between devices  37.6 us
    ppermute x8, starting transfers between devices, shifted_2(): lax.ppermute(value, axis, [(source, source + steps) for source in range(f...  19.5 us
    ppermute x8, waiting for transfers between devices, shifted_2(): lax.ppermute(value, axis, [(source, source + steps) for source in range(f...  13.4 us
    psum x1, blocking collectives, body(): along = lax.psum(dot_terms, 'tensor')  5.74 us
    dot_general x1, matrix products, body(): jnp.dot(attended, out_weight, preferred_element_type=jnp.float32)  5.74 us
    dot_general x1, matrix products, body(): jnp.einsum('kgqs,skd->qkgd', weights, every_value, preferred_element_type...  4.79 us
    unnamed x22, local copies, waits for them, and re-layouts  4.39 us
  transfers between devices with their start and end apart: 9, of which 4 were waited for; matrix products, arithmetic and copies ran while one was open for 7% of the time, Pallas kernels for 0%

commit v1 on v0

v1 whole, which is shorter than its diff:
```python
import functools

import jax
import jax.numpy as jnp
from jax import lax
from jax.experimental import pallas as pl
from jax.experimental.pallas import tpu as pltpu
from jax.sharding import PartitionSpec as P

HD = 256
HALF = HD // 2
WINDOW = 1024
NEG = -1e30


def rotary_tables(positions):
    freqs = jnp.power(10000.0, -jnp.arange(HALF, dtype=jnp.float32) * 2.0 / HD)
    angles = positions.astype(jnp.float32)[:, None] * freqs[None, :]
    return jnp.cos(angles), jnp.sin(angles)


def rotate(ref, head, cos, sin, scale=None):
    first = ref[:, head * HD : head * HD + HALF].astype(jnp.float32)
    second = ref[:, head * HD + HALF : (head + 1) * HD].astype(jnp.float32)
    low = first * cos - second * sin
    high = second * cos + first * sin
    if scale is not None:
        low, high = low * scale, high * scale
    return low.astype(jnp.bfloat16), high.astype(jnp.bfloat16)


def pack_kernel(key_ref, value_ref, cos_ref, sin_ref, *out_refs, per):
    cos, sin = cos_ref[...], sin_ref[...]
    for chunk, out_ref in enumerate(out_refs):
        for place in range(per):
            head = chunk * per + place
            low, high = rotate(key_ref, head, cos, sin)
            out_ref[:, place * HD : place * HD + HALF] = low
            out_ref[:, place * HD + HALF : (place + 1) * HD] = high
            out_ref[:, (per + place) * HD : (per + place + 1) * HD] = value_ref[
                :, head * HD : (head + 1) * HD
            ]


def rotate_queries_kernel(query_ref, cos_ref, sin_ref, out_ref, *, heads):
    cos, sin = cos_ref[...], sin_ref[...]
    for head in range(heads):
        low, high = rotate(query_ref, head, cos, sin, HD ** (-0.5))
        out_ref[:, head * HD : head * HD + HALF] = low
        out_ref[:, head * HD + HALF : (head + 1) * HD] = high


def attend_kernel(*refs, distances, chunks, per, group, has_state, finish):
    refs = list(refs)
    place_ref = refs.pop(0)
    query_ref = refs.pop(0)
    blocks = [[refs.pop(0) for _ in range(chunks)] for _ in distances]
    state_in = (refs.pop(0), refs.pop(0)) if has_state else None
    rows = query_ref.shape[0]
    lane = lax.broadcasted_iota(jnp.int32, (group * rows, 128), 1)
    gap = lax.broadcasted_iota(jnp.int32, (rows, rows), 0) - lax.broadcasted_iota(
        jnp.int32, (rows, rows), 1
    )
    gap = jnp.concatenate([gap] * group, axis=0)
    for kv in range(chunks * per):
        chunk, place = divmod(kv, per)
        query = jnp.concatenate(
            [query_ref[:, (kv * group + g) * HD : (kv * group + g + 1) * HD] for g in range(group)],
            axis=0,
        )
        all_scores = []
        for block, distance in zip(blocks, distances):
            keys = block[chunk][:, place * HD : (place + 1) * HD]
            scores = lax.dot_general(
                query, keys, (((1,), (1,)), ((), ())), preferred_element_type=jnp.float32
            )
            if distance == 0:
                scores = jnp.where(gap >= 0, scores, NEG)
            else:
                if distance * rows + rows - 1 >= WINDOW:
                    scores = jnp.where(gap + distance * rows < WINDOW, scores, NEG)
                scores = scores + jnp.where(place_ref[0] >= distance, 0.0, NEG)
            all_scores.append(scores)
        peak = functools.reduce(jnp.maximum, all_scores)
        peak = jnp.max(peak, axis=-1, keepdims=True)
        if has_state:
            stats = state_in[1][kv]
            old_peak = stats[:, :1]
            old_sum = stats[:, 64:65]
            peak = jnp.maximum(peak, old_peak)
            shrink = jnp.exp(old_peak - peak)
        total = None
        mixed = None
        for block, scores in zip(blocks, all_scores):
            weights = jnp.exp(scores - peak)
            part = jnp.sum(weights, axis=-1, keepdims=True)
            values = block[chunk][:, (per + place) * HD : (per + place + 1) * HD]
            moved = jnp.dot(
                weights.astype(jnp.bfloat16), values, preferred_element_type=jnp.float32
            )
            total = part if total is None else total + part
            mixed = moved if mixed is None else mixed + moved
        if has_state:
            total = total + old_sum * shrink
            mixed = mixed + state_in[0][kv] * shrink
        if finish:
            out_ref = refs[0]
            done = (mixed / total).astype(jnp.bfloat16)
            for g in range(group):
                out_ref[:, (kv * group + g) * HD : (kv * group + g + 1) * HD] = done[
                    g * rows : (g + 1) * rows
                ]
        else:
            refs[0][kv] = mixed
            refs[1][kv] = jnp.where(lane < 64, peak, total)


def attend(place, queries, blocks, distances, state, finish, per, group):
    rows, width = queries.shape
    chunks = len(blocks[0])
    kv_heads = chunks * per
    vmem = pl.BlockSpec(memory_space=pltpu.VMEM)
    smem = pl.BlockSpec(memory_space=pltpu.SMEM)
    flat = [chunk for block in blocks for chunk in block]
    extra = list(state) if state is not None else []
    if finish:
        out_shape = jax.ShapeDtypeStruct((rows, width), jnp.bfloat16)
        out_specs = vmem
    else:
        out_shape = (
            jax.ShapeDtypeStruct((kv_heads, group * rows, HD), jnp.float32),
            jax.ShapeDtypeStruct((kv_heads, group * rows, 128), jnp.float32),
        )
        out_specs = (vmem, vmem)
    kernel = functools.partial(
        attend_kernel,
        distances=tuple(distances),
        chunks=chunks,
        per=per,
        group=group,
        has_state=state is not None,
        finish=finish,
    )
    return pl.pallas_call(
        kernel,
        out_shape=out_shape,
        in_specs=[smem] + [vmem] * (1 + len(flat) + len(extra)),
        out_specs=out_specs,
        name="attend_" + "_".join(str(d) for d in distances),
    )(place, queries, *flat, *extra)


def body(queries, key_rows, value_rows, positions, residual, direction, out_weight):
    rows = queries.shape[0]
    heads = queries.shape[1] // HD
    kv_heads = key_rows.shape[1] // HD
    group = heads // kv_heads
    seq_size = lax.axis_size("seq")
    tensor_size = lax.axis_size("tensor")
    seq_index = lax.axis_index("seq")
    tensor_index = lax.axis_index("tensor")
    hops = min(-(-(WINDOW - 1) // rows), seq_size - 1)
    chunks = 2 if kv_heads % 2 == 0 else 1
    per = kv_heads // chunks
    vmem = pl.BlockSpec(memory_space=pltpu.VMEM)

    cos, sin = rotary_tables(positions)
    own = pl.pallas_call(
        functools.partial(pack_kernel, per=per),
        out_shape=[jax.ShapeDtypeStruct((rows, 2 * per * HD), jnp.bfloat16)] * chunks,
        in_specs=[vmem] * 4,
        out_specs=[vmem] * chunks,
        name="pack",
    )(key_rows, value_rows, cos, sin)

    up = [(source, source + 1) for source in range(seq_size - 1)]
    blocks = [list(own)]
    for _ in range(hops):
        blocks.append([lax.ppermute(chunk, "seq", up) for chunk in blocks[-1]])

    rot_queries = pl.pallas_call(
        functools.partial(rotate_queries_kernel, heads=heads),
        out_shape=jax.ShapeDtypeStruct(queries.shape, jnp.bfloat16),
        in_specs=[vmem] * 3,
        out_specs=vmem,
        name="rotate_queries",
    )(queries, cos, sin)
    place = seq_index.astype(jnp.int32).reshape(1)
    state = None
    for distance in range(hops + 1):
        state = attend(
            place, rot_queries, [blocks[distance]], [distance], state, distance == hops, per, group
        )
    attended = state

    column_width = residual.shape[1]
    unit_dir = direction / jnp.sqrt(jnp.sum(direction * direction) + 1e-06)
    local_dir = lax.dynamic_slice_in_dim(unit_dir, tensor_index * column_width, column_width, 0)
    base_state = residual.astype(jnp.float32)
    weight_along = jnp.sum(out_weight.astype(jnp.float32) * unit_dir[None, :], axis=1)
    along = jnp.sum(base_state * local_dir[None, :], axis=1) + jnp.sum(
        attended.astype(jnp.float32) * weight_along[None, :], axis=1
    )

    pieces = {}
    for r in reversed(range(tensor_size)):
        columns = lax.dynamic_slice_in_dim(
            out_weight, (tensor_index ^ r) * column_width, column_width, 1
        )
        pieces[r] = jnp.dot(attended, columns, preferred_element_type=jnp.float32)
    bit = 1
    while bit < tensor_size:
        swap = [(device, device ^ bit) for device in range(tensor_size)]
        for r in reversed(range(tensor_size)):
            if r & bit and not r & (bit - 1):
                arrived = lax.ppermute(pieces[r].astype(jnp.bfloat16), "tensor", swap)
                pieces[r ^ bit] = pieces[r ^ bit] + arrived.astype(jnp.float32)
        bit *= 2
    along = lax.psum(along, "tensor")
    hidden_state = base_state + pieces[0]
    return (hidden_state - along[:, None] * local_dir[None, :]).astype(jnp.bfloat16)


def solution(mesh):
    return jax.shard_map(
        body,
        mesh=mesh,
        in_specs=(
            P(("groups", "seq"), "tensor"),
            P(("groups", "seq"), "tensor"),
            P(("groups", "seq"), "tensor"),
            P(("groups", "seq")),
            P(("groups", "seq"), "tensor"),
            P("groups"),
            P("tensor", None),
        ),
        out_specs=P(("groups", "seq"), "tensor"),
        check_vma=False,
    )
```

time: 119 us -> 95 us (0.80)
  waiting for transfers between devices: 51.1 us -> 7.26 us
  Pallas kernels: 0 us -> 24.6 us
  between operations: 14.4 us -> 0.85 us
  starting transfers between devices: 19.5 us -> 28 us
  local copies, waits for them, and re-layouts: 6.64 us -> 0.87 us
  matrix products: 12.8 us -> 16 us
  blocking collectives: 5.74 us -> 8.91 us
    unnamed x2 -> x0, waiting for transfers between devices: 37.6 us -> none
    pallas_call x0 -> x6, Pallas kernels: none -> 24.6 us  [the longest x4 20.5 us: attend(): pl.pallas_call(kernel, out_shape=out_shape, in_specs=[smem] + [vmem] * (1...]
    ppermute x8 -> x9, starting transfers between devices: 19.5 us -> 28 us  [the longest x6 25.8 us: body(): blocks.append([lax.ppermute(chunk, 'seq', up) for chunk in blocks[-1]])]
    ppermute x8 -> x9, waiting for transfers between devices: 13.4 us -> 7.26 us  [the longest x6 7.25 us: body(): blocks.append([lax.ppermute(chunk, 'seq', up) for chunk in blocks[-1]])]
    reduce_sum x0 -> x2, other arithmetic: none -> 5.01 us  [the longest x1 4.83 us: body(): jnp.sum(out_weight.astype(jnp.float32) * unit_dir[None, :], axis=1)]
    unnamed x22 -> x18, local copies, waits for them, and re-layouts: 4.39 us -> 0.79 us
    dot_general x4, matrix products: 12.8 us -> 16 us  [body(): pieces[r] = jnp.dot(attended, columns, preferred_element_type=jnp.float32)]
    psum x1, blocking collectives: 5.74 us -> 8.91 us  [body(): along = lax.psum(along, 'tensor')]
  transfers between devices with their start and end apart: 9 -> 9, of which waited for: 4 -> 4; matrix products, arithmetic and copies ran while one was open for 7% -> 14% of each run, Pallas kernels for 0% -> 18%
where the time goes in v1:
time: 95 us; the launch traced here: 94.3 us
  starting transfers between devices  28 us (29%)
  Pallas kernels  24.6 us (26%)
  matrix products  16 us (17%)
  blocking collectives  8.91 us (9%)
  other arithmetic  7.78 us (8%)
  waiting for transfers between devices  7.26 us (8%)
    ppermute x6, starting transfers between devices, body(): blocks.append([lax.ppermute(chunk, 'seq', up) for chunk in blocks[-1]])  25.8 us
    pallas_call x4, Pallas kernels, attend(): pl.pallas_call(kernel, out_shape=out_shape, in_specs=[smem] + [vmem] * (1...  20.5 us
    dot_general x4, matrix products, body(): pieces[r] = jnp.dot(attended, columns, preferred_element_type=jnp.float32)  16 us
    psum x1, blocking collectives, body(): along = lax.psum(along, 'tensor')  8.91 us
    ppermute x6, waiting for transfers between devices, body(): blocks.append([lax.ppermute(chunk, 'seq', up) for chunk in blocks[-1]])  7.25 us
    reduce_sum x1, other arithmetic, body(): jnp.sum(out_weight.astype(jnp.float32) * unit_dir[None, :], axis=1)  4.83 us
    ppermute x3, starting transfers between devices, body(): arrived = lax.ppermute(pieces[r].astype(jnp.bfloat16), 'tensor', swap)  2.25 us
    pallas_call x1, Pallas kernels, body(): pl.pallas_call(functools.partial(rotate_queries_kernel, heads=heads), out...  2.19 us
  transfers between devices with their start and end apart: 9, of which 4 were waited for; matrix products, arithmetic and copies ran while one was open for 14% of the time, Pallas kernels for 18%

profile of v1, /device:TPU:0, one launch (start us, length us, event | category | flops | bytes accessed | tf_op | source)
XLA Modules:
  0.0 94.3 jit_solution(17462402486938726201)
XLA Ops:
  0.7 1.3 %multiply_sine_fusion = (f32[256,128]{1,0:T(8,128)}, f32[256,128]{1,0:T(8,128)}) fusion(f32[128]{0:T(128)S(1)} %multiply_power_fusion, f32[256]{0:T(256)S(1)} %convert_element_type.34), kind=kLoop, calls=%fused_computation.21 | loop fusion | flops 32768 | bytes 263680 | tf_op jit(solution)/shard_map/sin | solution.py:19
  2.0 2.0 %pack.1 = (bf16[256,512]{1,0:T(8,128)(2,1)}, bf16[256,512]{1,0:T(8,128)(2,1)}) custom-call(bf16[256,512]{1,0:T(8,128)(2,1)} %key_ref.1, bf16[256,512]{1,0:T(8,128)(2,1)} %value_ref.1, f32[256,128]{1,0:T(8,128)} %get-tuple-element.22.cos_ref, f32[256,128]{1,0:T(8,128)} %get-tuple-element.21.sin_ref), custom_call_target="tpu_custom_call" | custom-call | tf_op jit(solution)/shard_map/pack/pallas_call | solution.py:168
  3.9 5.0 %collective-permute-start = (bf16[256,512]{1,0:T(8,128)(2,1)}, bf16[256,512]{1,0:T(8,128)(2,1)S(1)}, u32[]{:S(2)}, u32[]{:S(2)}) collective-permute-start(bf16[256,512]{1,0:T(8,128)(2,1)} %get-tuple-element.13.refs_2_), channel_id=1, source_target_pairs={{0,4},{4,8},{8,12},{1,5},{5,9},{9,13},{2,6},{6,10},{10,14},{3,7},{... | collective-permute-start | bytes 786440 | tf_op jit(solution)/shard_map/ppermute | solution.py:179
  8.9 3.5 %collective-permute-start.3 = (bf16[256,512]{1,0:T(8,128)(2,1)}, bf16[256,512]{1,0:T(8,128)(2,1)S(1)}, u32[]{:S(2)}, u32[]{:S(2)}) collective-permute-start(bf16[256,512]{1,0:T(8,128)(2,1)} %get-tuple-element.14.refs_3_), channel_id=1, source_target_pairs={{0,4},{4,8},{8,12},{1,5},{5,9},{9,13},{2,6},{6,10},{10,14},{3,7},{... | collective-permute-start | bytes 786440 | tf_op jit(solution)/shard_map/ppermute | solution.py:179
  12.4 3.5 %collective-permute-done.refs_2_ = bf16[256,512]{1,0:T(8,128)(2,1)S(1)} collective-permute-done((bf16[256,512]{1,0:T(8,128)(2,1)}, bf16[256,512]{1,0:T(8,128)(2,1)S(1)}, u32[]{:S(2)}, u32[]{:S(2)}) %collective-permute-start) | collective-permute-done | bytes 262176 | tf_op jit(solution)/shard_map/ppermute | solution.py:179
  15.9 4.3 %collective-permute-start.1 = (bf16[256,512]{1,0:T(8,128)(2,1)S(1)}, bf16[256,512]{1,0:T(8,128)(2,1)S(1)}, u32[]{:S(2)}, u32[]{:S(2)}) collective-permute-start(bf16[256,512]{1,0:T(8,128)(2,1)S(1)} %collective-permute-done.refs_2_), channel_id=1, source_target_pairs={{0,4},{4,8},{8,12},{1,5},{5,9},{9,13},{2,6},{6,10},{10,14},{3,7},{... | collective-permute-start | bytes 786440 | tf_op jit(solution)/shard_map/ppermute | solution.py:179
  20.1 1.3 %collective-permute-done.3.refs_3_ = bf16[256,512]{1,0:T(8,128)(2,1)S(1)} collective-permute-done((bf16[256,512]{1,0:T(8,128)(2,1)}, bf16[256,512]{1,0:T(8,128)(2,1)S(1)}, u32[]{:S(2)}, u32[]{:S(2)}) %collective-permute-start.3) | collective-permute-done | bytes 262176 | tf_op jit(solution)/shard_map/ppermute | solution.py:179
  21.5 4.3 %collective-permute-start.4 = (bf16[256,512]{1,0:T(8,128)(2,1)S(1)}, bf16[256,512]{1,0:T(8,128)(2,1)S(1)}, u32[]{:S(2)}, u32[]{:S(2)}) collective-permute-start(bf16[256,512]{1,0:T(8,128)(2,1)S(1)} %collective-permute-done.3.refs_3_), channel_id=1, source_target_pairs={{0,4},{4,8},{8,12},{1,5},{5,9},{9,13},{2,6},{6,10},{10,14},{3,7},{... | collective-permute-start | bytes 786440 | tf_op jit(solution)/shard_map/ppermute | solution.py:179
  25.8 1.2 %collective-permute-done.1.refs_2_ = bf16[256,512]{1,0:T(8,128)(2,1)S(1)} collective-permute-done((bf16[256,512]{1,0:T(8,128)(2,1)S(1)}, bf16[256,512]{1,0:T(8,128)(2,1)S(1)}, u32[]{:S(2)}, u32[]{:S(2)}) %collective-permute-start.1) | collective-permute-done | bytes 262176 | tf_op jit(solution)/shard_map/ppermute | solution.py:179
  27.0 4.4 %collective-permute-start.2 = (bf16[256,512]{1,0:T(8,128)(2,1)S(1)}, bf16[256,512]{1,0:T(8,128)(2,1)S(1)}, u32[]{:S(2)}, u32[]{:S(2)}) collective-permute-start(bf16[256,512]{1,0:T(8,128)(2,1)S(1)} %collective-permute-done.1.refs_2_), channel_id=1, source_target_pairs={{0,4},{4,8},{8,12},{1,5},{5,9},{9,13},{2,6},{6,10},{10,14},{3,7},{... | collective-permute-start | bytes 786440 | tf_op jit(solution)/shard_map/ppermute | solution.py:179
  31.4 1.2 %collective-permute-done.4.refs_3_ = bf16[256,512]{1,0:T(8,128)(2,1)S(1)} collective-permute-done((bf16[256,512]{1,0:T(8,128)(2,1)S(1)}, bf16[256,512]{1,0:T(8,128)(2,1)S(1)}, u32[]{:S(2)}, u32[]{:S(2)}) %collective-permute-start.4) | collective-permute-done | bytes 262176 | tf_op jit(solution)/shard_map/ppermute | solution.py:179
  32.6 4.4 %collective-permute-start.5 = (bf16[256,512]{1,0:T(8,128)(2,1)S(1)}, bf16[256,512]{1,0:T(8,128)(2,1)S(1)}, u32[]{:S(2)}, u32[]{:S(2)}) collective-permute-start(bf16[256,512]{1,0:T(8,128)(2,1)S(1)} %collective-permute-done.4.refs_3_), channel_id=1, source_target_pairs={{0,4},{4,8},{8,12},{1,5},{5,9},{9,13},{2,6},{6,10},{10,14},{3,7},{... | collective-permute-start | bytes 786440 | tf_op jit(solution)/shard_map/ppermute | solution.py:179
  37.0 2.2 %rotate_queries.1.refs_1_ = bf16[256,1024]{1,0:T(8,128)(2,1)} custom-call(bf16[256,1024]{1,0:T(8,128)(2,1)} %query_ref.1, f32[256,128]{1,0:T(8,128)} %get-tuple-element.22.cos_ref, f32[256,128]{1,0:T(8,128)} %get-tuple-element.21.sin_ref), custom_call_target="tpu_custom_call" | custom-call | tf_op jit(solution)/shard_map/rotate_queries/pallas_call | solution.py:181
  39.2 3.2 %attend_0.1 = (f32[2,512,256]{2,1,0:T(8,128)}, f32[2,512,128]{2,1,0:T(8,128)}) custom-call(s32[1]{0:T(128)} %bitcast.refs_0_, bf16[256,1024]{1,0:T(8,128)(2,1)} %rotate_queries.1.refs_1_, bf16[256,512]{1,0:T(8,128)(2,1)} %get-tuple-element.13.refs_2_, bf16[256,512]{1,0:T(8,128)(2,1)} %get-tuple-element.14.refs_3_), custom_call_target="tpu_custom_call" | custom-call | tf_op jit(solution)/shard_map/attend_0/pallas_call | solution.py:144
  42.4 5.7 %attend_1.1 = (f32[2,512,256]{2,1,0:T(8,128)}, f32[2,512,128]{2,1,0:T(8,128)}) custom-call(s32[1]{0:T(128)} %bitcast.refs_0_, bf16[256,1024]{1,0:T(8,128)(2,1)} %rotate_queries.1.refs_1_, bf16[256,512]{1,0:T(8,128)(2,1)} %copy-done.2, bf16[256,512]{1,0:T(8,128)(2,1)} %copy-done.4, f32[2,512,256]{2,1,0:T(8,128)} %get-tuple-element.15.refs_4_, ...), custom_call_target="tpu_custom_call" | custom-call | tf_op jit(solution)/shard_map/attend_1/pallas_call | solution.py:144
  48.2 5.7 %attend_2.1 = (f32[2,512,256]{2,1,0:T(8,128)}, f32[2,512,128]{2,1,0:T(8,128)}) custom-call(s32[1]{0:T(128)} %bitcast.refs_0_, bf16[256,1024]{1,0:T(8,128)(2,1)} %rotate_queries.1.refs_1_, bf16[256,512]{1,0:T(8,128)(2,1)} %copy-done.3, bf16[256,512]{1,0:T(8,128)(2,1)} %copy-done.5, f32[2,512,256]{2,1,0:T(8,128)} %get-tuple-element.17.refs_4_, ...), custom_call_target="tpu_custom_call" | custom-call | tf_op jit(solution)/shard_map/attend_2/pallas_call | solution.py:144
  54.7 5.7 %attend_3.1 = bf16[256,1024]{1,0:T(8,128)(2,1)} custom-call(s32[1]{0:T(128)} %bitcast.refs_0_, bf16[256,1024]{1,0:T(8,128)(2,1)} %rotate_queries.1.refs_1_, bf16[256,512]{1,0:T(8,128)(2,1)} %copy-done.6, bf16[256,512]{1,0:T(8,128)(2,1)} %copy-done.7, f32[2,512,256]{2,1,0:T(8,128)} %get-tuple-element.19.refs_4_, f32[2,512,128]{2,1,0:T(8,128)} %get-tuple-element.20.refs_5_), custom_call_target="tpu_custom_call" | custom-call | tf_op jit(solution)/shard_map/attend_3/pallas_call | solution.py:144
  60.4 3.7 %fusion.32 = bf16[256,960]{0,1:T(8,128)(2,1)S(1)} fusion(bf16[256,1024]{1,0:T(8,128)(2,1)} %attend_3.1, bf16[1024,3840]{1,0:T(8,128)(2,1)} %param.13, s32[]{:T(128)S(6)} %select_n.16), kind=kOutput, calls=%fused_computation.17 | convolution fusion | flops 503562240 | bytes 3112964 | tf_op jit(solution)/shard_map/dot_general | solution.py:210
  65.6 3.8 %fusion.29 = bf16[256,960]{0,1:T(8,128)(2,1)S(1)} fusion(bf16[256,1024]{1,0:T(8,128)(2,1)} %attend_3.1, bf16[1024,3840]{1,0:T(8,128)(2,1)} %param.13, s32[]{:T(128)S(6)} %select_n.14), kind=kOutput, calls=%fused_computation.16 | convolution fusion | flops 503562240 | bytes 3112964 | tf_op jit(solution)/shard_map/dot_general | solution.py:210
  69.9 4.0 %fusion.23 = bf16[256,960]{0,1:T(8,128)(2,1)S(1)} fusion(bf16[256,1024]{1,0:T(8,128)(2,1)} %attend_3.1, bf16[1024,3840]{1,0:T(8,128)(2,1)} %param.13, s32[]{:T(128)S(6)} %select_n.15, bf16[256,960]{0,1:T(8,128)(2,1)S(1)} %collective-permute-done.7), kind=kOutput, calls=%fused_computation.14 | convolution fusion | flops 504053760 | bytes 3604484 | tf_op jit(solution)/shard_map/dot_general | solution.py:210
  73.9 1.6 %collective-permute-start.8 = (bf16[256,960]{0,1:T(8,128)(2,1)S(1)}, bf16[256,960]{0,1:T(8,128)(2,1)S(1)}, u32[]{:S(2)}, u32[]{:S(2)}) collective-permute-start(bf16[256,960]{0,1:T(8,128)(2,1)S(1)} %fusion.23), channel_id=1, source_target_pairs={{0,2},{1,3},{2,0},{3,1},{4,6},{5,7},{6,4},{7,5},{8,10},{9,11},{10,... | collective-permute-start | bytes 1474568 | tf_op jit(solution)/shard_map/ppermute | solution.py:216
  75.5 4.8 %multiply_reduce_fusion = f32[1024]{0:T(1024)S(1)} fusion(bf16[1024,3840]{1,0:T(8,128)(2,1)} %param.13, f32[3840]{0:T(1024)S(1)} %broadcast_divide_fusion), kind=kLoop, calls=%fused_computation | loop fusion | flops 11795456 | bytes 7883776 | tf_op jit(solution)/shard_map/reduce_sum | solution.py:200
  80.8 8.9 %psum.7 = f32[256]{0:T(256)S(1)} all-reduce(f32[256]{0:T(256)S(1)} %add.42), channel_id=1, replica_groups=mesh['groups'=2,'seq'=4,'tensor'=4] {'tensor'}, use_global_device_ids=true, to_apply=%region_4.0 | all-reduce | flops 256 | bytes 2048 | tf_op jit(solution)/shard_map/psum | solution.py:219
  89.7 4.6 %fusion.26 = bf16[256,960]{0,1:T(8,128)(2,1)} fusion(bf16[256,1024]{1,0:T(8,128)(2,1)S(1)} %copy-done, bf16[1024,3840]{1,0:T(8,128)(2,1)} %param.13, s32[]{:T(128)S(6)} %select_n.13, bf16[256,960]{0,1:T(8,128)(2,1)S(1)} %copy-done.1, bf16[256,960]{0,1:T(8,128)(2,1)S(1)} %collective-permute-done.8, bf16[256,960]{0,1:T(8,128)(2,1)S(1)} %collective-permute-done.6, ...), kind=kOutput, calls=%fused_computation.15 | convolution fusion | flops 505528320 | bytes 4592388 | tf_op jit(solution)/shard_map/dot_general | solution.py:210
  (33 shorter events, 3.2 us)
Async XLA Ops:
  0.0 64.2 %copy-start.8 = (f32[3840]{0:T(1024)S(1)}, f32[3840]{0:T(1024)}, u32[]{:S(2)}) copy-start(f32[3840]{0:T(1024)} %param.12) | copy-start | bytes 46084
  3.9 11.9 %collective-permute-start = (bf16[256,512]{1,0:T(8,128)(2,1)}, bf16[256,512]{1,0:T(8,128)(2,1)S(1)}, u32[]{:S(2)}, u32[]{:S(2)}) collective-permute-start(bf16[256,512]{1,0:T(8,128)(2,1)} %get-tuple-element.13.refs_2_), channel_id=1, source_target_pairs={{0,4},{4,8},{8,12},{1,5},{5,9},{9,13},{2,6},{6,10},{10,14},{3,7},{... | collective-permute-start | bytes 786440 | tf_op jit(solution)/shard_map/ppermute | solution.py:179
  8.9 12.6 %collective-permute-start.3 = (bf16[256,512]{1,0:T(8,128)(2,1)}, bf16[256,512]{1,0:T(8,128)(2,1)S(1)}, u32[]{:S(2)}, u32[]{:S(2)}) collective-permute-start(bf16[256,512]{1,0:T(8,128)(2,1)} %get-tuple-element.14.refs_3_), channel_id=1, source_target_pairs={{0,4},{4,8},{8,12},{1,5},{5,9},{9,13},{2,6},{6,10},{10,14},{3,7},{... | collective-permute-start | bytes 786440 | tf_op jit(solution)/shard_map/ppermute | solution.py:179
  15.9 26.6 %copy-start.2 = (bf16[256,512]{1,0:T(8,128)(2,1)}, bf16[256,512]{1,0:T(8,128)(2,1)S(1)}, u32[]{:S(2)}) copy-start(bf16[256,512]{1,0:T(8,128)(2,1)S(1)} %collective-permute-done.refs_2_) | copy-start | bytes 786436
  15.9 11.1 %collective-permute-start.1 = (bf16[256,512]{1,0:T(8,128)(2,1)S(1)}, bf16[256,512]{1,0:T(8,128)(2,1)S(1)}, u32[]{:S(2)}, u32[]{:S(2)}) collective-permute-start(bf16[256,512]{1,0:T(8,128)(2,1)S(1)} %collective-permute-done.refs_2_), channel_id=1, source_target_pairs={{0,4},{4,8},{8,12},{1,5},{5,9},{9,13},{2,6},{6,10},{10,14},{3,7},{... | collective-permute-start | bytes 786440 | tf_op jit(solution)/shard_map/ppermute | solution.py:179
  21.5 21.0 %copy-start.4 = (bf16[256,512]{1,0:T(8,128)(2,1)}, bf16[256,512]{1,0:T(8,128)(2,1)S(1)}, u32[]{:S(2)}) copy-start(bf16[256,512]{1,0:T(8,128)(2,1)S(1)} %collective-permute-done.3.refs_3_) | copy-start | bytes 786436
  21.5 11.1 %collective-permute-start.4 = (bf16[256,512]{1,0:T(8,128)(2,1)S(1)}, bf16[256,512]{1,0:T(8,128)(2,1)S(1)}, u32[]{:S(2)}, u32[]{:S(2)}) collective-permute-start(bf16[256,512]{1,0:T(8,128)(2,1)S(1)} %collective-permute-done.3.refs_3_), channel_id=1, source_target_pairs={{0,4},{4,8},{8,12},{1,5},{5,9},{9,13},{2,6},{6,10},{10,14},{3,7},{... | collective-permute-start | bytes 786440 | tf_op jit(solution)/shard_map/ppermute | solution.py:179
  27.0 21.2 %copy-start.3 = (bf16[256,512]{1,0:T(8,128)(2,1)}, bf16[256,512]{1,0:T(8,128)(2,1)S(1)}, u32[]{:S(2)}) copy-start(bf16[256,512]{1,0:T(8,128)(2,1)S(1)} %collective-permute-done.1.refs_2_) | copy-start | bytes 786436
  27.0 26.9 %collective-permute-start.2 = (bf16[256,512]{1,0:T(8,128)(2,1)S(1)}, bf16[256,512]{1,0:T(8,128)(2,1)S(1)}, u32[]{:S(2)}, u32[]{:S(2)}) collective-permute-start(bf16[256,512]{1,0:T(8,128)(2,1)S(1)} %collective-permute-done.1.refs_2_), channel_id=1, source_target_pairs={{0,4},{4,8},{8,12},{1,5},{5,9},{9,13},{2,6},{6,10},{10,14},{3,7},{... | collective-permute-start | bytes 786440 | tf_op jit(solution)/shard_map/ppermute | solution.py:179
  32.6 15.6 %copy-start.5 = (bf16[256,512]{1,0:T(8,128)(2,1)}, bf16[256,512]{1,0:T(8,128)(2,1)S(1)}, u32[]{:S(2)}) copy-start(bf16[256,512]{1,0:T(8,128)(2,1)S(1)} %collective-permute-done.4.refs_3_) | copy-start | bytes 786436
  32.6 21.3 %collective-permute-start.5 = (bf16[256,512]{1,0:T(8,128)(2,1)S(1)}, bf16[256,512]{1,0:T(8,128)(2,1)S(1)}, u32[]{:S(2)}, u32[]{:S(2)}) collective-permute-start(bf16[256,512]{1,0:T(8,128)(2,1)S(1)} %collective-permute-done.4.refs_3_), channel_id=1, source_target_pairs={{0,4},{4,8},{8,12},{1,5},{5,9},{9,13},{2,6},{6,10},{10,14},{3,7},{... | collective-permute-start | bytes 786440 | tf_op jit(solution)/shard_map/ppermute | solution.py:179
  53.9 0.7 copy-start.6
  53.9 0.8 copy-start.7
  64.1 16.3 %copy-start.1 = (bf16[256,960]{0,1:T(8,128)(2,1)S(1)}, bf16[256,960]{0,1:T(8,128)(2,1)}, u32[]{:S(2)}) copy-start(bf16[256,960]{0,1:T(8,128)(2,1)} %param.11) | copy-start | bytes 1474564
  64.2 16.5 %copy-start = (bf16[256,1024]{1,0:T(8,128)(2,1)S(1)}, bf16[256,1024]{1,0:T(8,128)(2,1)}, u32[]{:S(2)}) copy-start(bf16[256,1024]{1,0:T(8,128)(2,1)} %attend_3.1) | copy-start | bytes 1572868
  64.2 5.7 %collective-permute-start.7 = (bf16[256,960]{0,1:T(8,128)(2,1)S(1)}, bf16[256,960]{0,1:T(8,128)(2,1)S(1)}, u32[]{:S(2)}, u32[]{:S(2)}) collective-permute-start(bf16[256,960]{0,1:T(8,128)(2,1)S(1)} %fusion.32), channel_id=1, source_target_pairs={{0,1},{1,0},{2,3},{3,2},{4,5},{5,4},{6,7},{7,6},{8,9},{9,8},{10,11... | collective-permute-start | bytes 1474568 | tf_op jit(solution)/shard_map/ppermute | solution.py:216
  69.4 20.4 %collective-permute-start.6 = (bf16[256,960]{0,1:T(8,128)(2,1)S(1)}, bf16[256,960]{0,1:T(8,128)(2,1)S(1)}, u32[]{:S(2)}, u32[]{:S(2)}) collective-permute-start(bf16[256,960]{0,1:T(8,128)(2,1)S(1)} %fusion.29), channel_id=1, source_target_pairs={{0,1},{1,0},{2,3},{3,2},{4,5},{5,4},{6,7},{7,6},{8,9},{9,8},{10,11... | collective-permute-start | bytes 1474568 | tf_op jit(solution)/shard_map/ppermute | solution.py:216
  73.9 15.9 %collective-permute-start.8 = (bf16[256,960]{0,1:T(8,128)(2,1)S(1)}, bf16[256,960]{0,1:T(8,128)(2,1)S(1)}, u32[]{:S(2)}, u32[]{:S(2)}) collective-permute-start(bf16[256,960]{0,1:T(8,128)(2,1)S(1)} %fusion.23), channel_id=1, source_target_pairs={{0,2},{1,3},{2,0},{3,1},{4,6},{5,7},{6,4},{7,5},{8,10},{9,11},{10,... | collective-permute-start | bytes 1474568 | tf_op jit(solution)/shard_map/ppermute | solution.py:216

commit v2 on v1

v2 whole, which is shorter than its diff:
```python
import functools

import jax
import jax.numpy as jnp
from jax import lax
from jax.experimental import pallas as pl
from jax.experimental.pallas import tpu as pltpu
from jax.sharding import PartitionSpec as P

HD = 256
HALF = HD // 2
WINDOW = 1024
NEG = -1e30
F32 = jnp.float32
BF16 = jnp.bfloat16


def run(kernel, scalars, arrays, outs, name, scratch=()):
    smem = pl.BlockSpec(memory_space=pltpu.SMEM)
    vmem = pl.BlockSpec(memory_space=pltpu.VMEM)
    single = len(outs) == 1
    shapes = [pltpu.VMEM(shape, dtype) for shape, dtype in outs]
    return pl.pallas_call(
        kernel,
        out_shape=shapes[0] if single else shapes,
        in_specs=[smem] * len(scalars) + [vmem] * len(arrays),
        out_specs=vmem if single else [vmem] * len(outs),
        scratch_shapes=list(scratch),
        compiler_params=pltpu.CompilerParams(vmem_limit_bytes=24 * 2**20),
        name=name,
    )(*scalars, *[pltpu.with_memory_space_constraint(a, pltpu.VMEM) for a in arrays])


def after(value, *others):
    return lax.optimization_barrier((value, *others))[0]


def rotary_tables(positions):
    freqs = jnp.power(10000.0, -jnp.arange(HALF, dtype=F32) * 2.0 / HD)
    angles = positions.astype(F32)[:, None] * freqs[None, :]
    return jnp.cos(angles), jnp.sin(angles)


def rotate_kernel(ref, cos_ref, sin_ref, out_ref, *, scale):
    cos, sin = cos_ref[...], sin_ref[...]
    for head in range(ref.shape[1] // HD):
        first = ref[:, head * HD : head * HD + HALF].astype(F32)
        second = ref[:, head * HD + HALF : (head + 1) * HD].astype(F32)
        low = first * cos - second * sin
        high = second * cos + first * sin
        if scale is not None:
            low, high = low * scale, high * scale
        out_ref[:, head * HD : head * HD + HALF] = low.astype(BF16)
        out_ref[:, head * HD + HALF : (head + 1) * HD] = high.astype(BF16)


def rotate(block, cos, sin, scale, name):
    kernel = functools.partial(rotate_kernel, scale=scale)
    return run(kernel, (), (block, cos, sin), [(block.shape, BF16)], name)


def attend_kernel(*refs, distances, group, has_state, finish):
    refs = list(refs)
    place_ref = refs.pop(0)
    query_ref = refs.pop(0)
    blocks = [(refs.pop(0), refs.pop(0)) for _ in distances]
    state_in = (refs.pop(0), refs.pop(0)) if has_state else None
    rows = query_ref.shape[0]
    lane = lax.broadcasted_iota(jnp.int32, (group * rows, 128), 1)
    gap = lax.broadcasted_iota(jnp.int32, (rows, rows), 0) - lax.broadcasted_iota(
        jnp.int32, (rows, rows), 1
    )
    gap = jnp.concatenate([gap] * group, axis=0)
    for kv in range(query_ref.shape[1] // (group * HD)):
        mine = slice(kv * HD, (kv + 1) * HD)
        query = jnp.concatenate(
            [query_ref[:, (kv * group + g) * HD : (kv * group + g + 1) * HD] for g in range(group)],
            axis=0,
        )
        all_scores = []
        for (key_ref, _), distance in zip(blocks, distances):
            scores = lax.dot_general(
                query, key_ref[:, mine], (((1,), (1,)), ((), ())), preferred_element_type=F32
            )
            if distance == 0:
                scores = jnp.where(gap >= 0, scores, NEG)
            else:
                if distance * rows + rows - 1 >= WINDOW:
                    scores = jnp.where(gap + distance * rows < WINDOW, scores, NEG)
                scores = scores + jnp.where(place_ref[0] >= distance, 0.0, NEG)
            all_scores.append(scores)
        peak = functools.reduce(jnp.maximum, all_scores)
        peak = jnp.max(peak, axis=-1, keepdims=True)
        if has_state:
            stats = state_in[1][kv]
            old_peak = stats[:, :1]
            old_sum = stats[:, 64:65]
            peak = jnp.maximum(peak, old_peak)
            shrink = jnp.exp(old_peak - peak)
        total = None
        mixed = None
        for (_, value_ref), scores in zip(blocks, all_scores):
            weights = jnp.exp(scores - peak)
            part = jnp.sum(weights, axis=-1, keepdims=True)
            moved = jnp.dot(weights.astype(BF16), value_ref[:, mine], preferred_element_type=F32)
            total = part if total is None else total + part
            mixed = moved if mixed is None else mixed + moved
        if has_state:
            total = total + old_sum * shrink
            mixed = mixed + state_in[0][kv] * shrink
        if finish:
            done = (mixed / total).astype(BF16)
            for g in range(group):
                refs[0][:, (kv * group + g) * HD : (kv * group + g + 1) * HD] = done[
                    g * rows : (g + 1) * rows
                ]
        else:
            refs[0][kv] = mixed
            refs[1][kv] = jnp.where(lane < 64, peak, total)


def attend(place, queries, blocks, distances, state, finish, group):
    rows, width = queries.shape
    kv_heads = width // (group * HD)
    if finish:
        outs = [((rows, width), BF16)]
    else:
        outs = [((kv_heads, group * rows, HD), F32), ((kv_heads, group * rows, 128), F32)]
    kernel = functools.partial(
        attend_kernel,
        distances=tuple(distances),
        group=group,
        has_state=state is not None,
        finish=finish,
    )
    arrays = [queries, *[part for block in blocks for part in block], *(state or ())]
    return run(kernel, (place,), arrays, outs, "attend_" + "_".join(map(str, distances)))


def split3(value):
    high = value.astype(BF16)
    rest = value - high.astype(F32)
    middle = rest.astype(BF16)
    return high, middle, (rest - middle.astype(F32)).astype(BF16)


def terms8(value):
    rows = lax.broadcasted_iota(jnp.int32, (8, value.shape[1]), 0)
    high, middle, low = (term.astype(F32) for term in split3(value))
    return jnp.where(
        rows == 0, high, jnp.where(rows == 1, middle, jnp.where(rows == 2, low, 0.0))
    ).astype(BF16)


def add3(rows):
    return rows[0:1].astype(F32) + rows[1:2].astype(F32) + rows[2:3].astype(F32)


def direction_kernel(unit_ref, weight_ref, out_ref):
    product = lax.dot_general(
        terms8(unit_ref[...]),
        weight_ref[...],
        (((1,), (1,)), ((), ())),
        preferred_element_type=F32,
    )
    out_ref[...] = terms8(add3(product))


def residual_kernel(local_ref, residual_ref, out_ref):
    product = jnp.dot(terms8(local_ref[...]), residual_ref[...], preferred_element_type=F32)
    out_ref[...] = add3(product)


def project_kernel(*refs, width, with_along):
    refs = list(refs)
    where_ref, attended_ref, weight_ref = refs[:3]
    start = pl.multiple_of(where_ref[0], 128)
    half = 2 * width
    product = jnp.dot(
        attended_ref[...], weight_ref[:, pl.ds(start, half)], preferred_element_type=F32
    )
    if with_along:
        direction_ref, residual_ref, send_ref, keep_ref, along_ref, scratch = refs[3:]
    else:
        send_ref, keep_ref, scratch = refs[3:]
    scratch[...] = product.T
    keep_ref[...] = scratch[pl.ds(pl.multiple_of(where_ref[1], 8), width), :]
    send_ref[:width, :] = scratch[pl.ds(pl.multiple_of(where_ref[2], 8), width), :].astype(BF16)
    if with_along:
        along = residual_ref[...] + add3(
            lax.dot_general(
                direction_ref[...],
                attended_ref[...],
                (((1,), (1,)), ((), ())),
                preferred_element_type=F32,
            )
        )
        along_ref[...] = along
        send_ref[width:, :] = jnp.concatenate([terms8(along), jnp.zeros_like(terms8(along))], 0)


def pair_kernel(keep_ref, along_ref, came_ref, send_ref, along_out_ref):
    width = keep_ref.shape[0]
    send_ref[:width, :] = (keep_ref[...] + came_ref[:width, :].astype(F32)).astype(BF16)
    along = along_ref[...] + add3(came_ref[width : width + 8, :])
    along_out_ref[...] = along
    send_ref[width:, :] = jnp.concatenate([terms8(along), jnp.zeros_like(terms8(along))], 0)


def own_kernel(residual_ref, keep_ref, came_ref, out_ref):
    out_ref[...] = residual_ref[...].astype(F32) + keep_ref[...] + came_ref[...].astype(F32)


def final_kernel(own_ref, along_ref, came_ref, local_ref, out_ref):
    width = own_ref.shape[0]
    along = along_ref[...] + add3(came_ref[width : width + 8, :])
    hidden = own_ref[...] + came_ref[:width, :].astype(F32)
    out_ref[...] = (hidden - local_ref[...] * along).astype(BF16)


def unit_direction(direction):
    return direction / jnp.sqrt(jnp.sum(direction * direction) + 1e-06)


def local_part(unit, width):
    return lax.dynamic_slice_in_dim(unit, lax.axis_index("tensor") * width, width, 0)


def four_way_tail(attended, prepared, residual, out_weight):
    rows, width = residual.shape
    local_row, local_column, along_weight, residual_along = prepared
    tensor_index = lax.axis_index("tensor")
    core, chip = tensor_index % 2, tensor_index // 2
    far = jnp.stack([(1 - chip) * 2 * width, core * width, (1 - core) * width]).astype(jnp.int32)
    near = jnp.stack([chip * 2 * width, core * width, (1 - core) * width]).astype(jnp.int32)
    core_swap = [(0, 1), (1, 0), (2, 3), (3, 2)]
    chip_swap = [(0, 2), (2, 0), (1, 3), (3, 1)]
    scratch = [pltpu.VMEM((2 * width, rows), F32)]
    send, keep, along = run(
        functools.partial(project_kernel, width=width, with_along=True),
        (far,),
        (attended, out_weight, along_weight, residual_along),
        [((width + 16, rows), BF16), ((width, rows), F32), ((1, rows), F32)],
        "project_far",
        scratch,
    )
    came = lax.ppermute(send, "tensor", core_swap)
    send, along = run(
        pair_kernel,
        (),
        (keep, along, came),
        [((width + 16, rows), BF16), ((1, rows), F32)],
        "pair",
    )
    came_far = lax.ppermute(send, "tensor", chip_swap)
    send_near, keep_near = run(
        functools.partial(project_kernel, width=width, with_along=False),
        (near,),
        (after(attended, send), out_weight),
        [((width, rows), BF16), ((width, rows), F32)],
        "project_near",
        scratch,
    )
    came_near = lax.ppermute(send_near, "tensor", core_swap)
    own = run(
        own_kernel, (), (residual.T, keep_near, came_near), [((width, rows), F32)], "own"
    )
    out = run(
        final_kernel, (), (own, along, came_far, local_column), [((width, rows), BF16)], "final"
    )
    return out.T


def general_tail(attended, unit, residual, out_weight):
    width = residual.shape[1]
    tensor_size = lax.axis_size("tensor")
    tensor_index = lax.axis_index("tensor")
    local_dir = local_part(unit, width)
    base_state = residual.astype(F32)
    weight_along = jnp.sum(out_weight.astype(F32) * unit[None, :], axis=1)
    along = jnp.sum(base_state * local_dir[None, :], axis=1) + jnp.sum(
        attended.astype(F32) * weight_along[None, :], axis=1
    )
    pieces = {}
    for r in reversed(range(tensor_size)):
        columns = lax.dynamic_slice_in_dim(out_weight, (tensor_index ^ r) * width, width, 1)
        pieces[r] = jnp.dot(attended, columns, preferred_element_type=F32)
    bit = 1
    while bit < tensor_size:
        swap = [(device, device ^ bit) for device in range(tensor_size)]
        for r in reversed(range(tensor_size)):
            if r & bit and not r & (bit - 1):
                arrived = lax.ppermute(pieces[r].astype(BF16), "tensor", swap)
                pieces[r ^ bit] = pieces[r ^ bit] + arrived.astype(F32)
        bit *= 2
    along = lax.psum(along, "tensor")
    return (base_state + pieces[0] - along[:, None] * local_dir[None, :]).astype(BF16)


def body(queries, key_rows, value_rows, positions, residual, direction, out_weight):
    rows, width = residual.shape
    group = queries.shape[1] // key_rows.shape[1]
    seq_size = lax.axis_size("seq")
    tensor_size = lax.axis_size("tensor")
    hops = min(-(-(WINDOW - 1) // rows), seq_size - 1)
    four_way = tensor_size == 4 and width % 64 == 0
    place = lax.axis_index("seq").astype(jnp.int32).reshape(1)

    up = [(source, source + 1) for source in range(seq_size - 1)]
    values = [value_rows]
    keys = []
    cos, sin = rotary_tables(positions)
    keys.append(rotate(key_rows, cos, sin, None, "rotate_keys"))
    rot_queries = rotate(queries, cos, sin, HD ** (-0.5), "rotate_queries")
    state = None
    for distance in range(1, hops + 1):
        values.append(lax.ppermute(values[-1], "seq", up))
        last = keys[-1] if state is None else after(keys[-1], *state)
        keys.append(lax.ppermute(last, "seq", up))
        state = attend(
            place,
            rot_queries,
            [(keys[distance - 1], values[distance - 1])],
            [distance - 1],
            state,
            False,
            group,
        )

    unit = unit_direction(direction)
    if four_way:
        local = local_part(unit, width)
        prepared = (
            local.reshape(1, width),
            local.reshape(width, 1),
            run(direction_kernel, (), (unit.reshape(1, -1), out_weight), [((8, out_weight.shape[0]), BF16)], "direction"),
            run(residual_kernel, (), (local.reshape(1, width), residual.T), [((1, rows), F32)], "residual_along"),
        )
        *prepared, state0, state1 = lax.optimization_barrier((*prepared, *state))
        state = (state0, state1)
    attended = attend(
        place, rot_queries, [(keys[hops], values[hops])], [hops], state, True, group
    )
    if four_way:
        return four_way_tail(attended, prepared, residual, out_weight)
    return general_tail(attended, unit, residual, out_weight)


def solution(mesh):
    return jax.shard_map(
        body,
        mesh=mesh,
        in_specs=(
            P(("groups", "seq"), "tensor"),
            P(("groups", "seq"), "tensor"),
            P(("groups", "seq"), "tensor"),
            P(("groups", "seq")),
            P(("groups", "seq"), "tensor"),
            P("groups"),
            P("tensor", None),
        ),
        out_specs=P(("groups", "seq"), "tensor"),
        check_vma=False,
    )
```

time: 95 us -> 76 us (0.80)
  matrix products: 16 us -> 0 us
  local copies, waits for them, and re-layouts: 0.87 us -> 15.6 us
  blocking collectives: 8.91 us -> 0 us
  other arithmetic: 7.78 us -> 3.49 us
  Pallas kernels: 24.6 us -> 20.7 us
  starting transfers between devices: 28 us -> 26.2 us
  waiting for transfers between devices: 7.26 us -> 8.56 us
    dot_general x4 -> x0, matrix products: 16 us -> none  [body(): pieces[r] = jnp.dot(attended, columns, preferred_element_type=jnp.float32)]
    unnamed x18 -> x21, local copies, waits for them, and re-layouts: 0.79 us -> 15.3 us
    psum x1 -> x0, blocking collectives: 8.91 us -> none  [body(): along = lax.psum(along, 'tensor')]
    reduce_sum x4 -> x1, other arithmetic: 5.83 us -> 1.39 us  [unit_direction(): return direction / jnp.sqrt(jnp.sum(direction * direction) + 1e-06)]
    pallas_call x6 -> x13, Pallas kernels: 24.6 us -> 20.7 us  [run(): pl.pallas_call(kernel, out_shape=shapes[0] if single else shapes, in_spec...]
    ppermute x9, starting transfers between devices: 28 us -> 26.2 us  [the longest x3 12.3 us: body(): keys.append(lax.ppermute(last, 'seq', up))]
    ppermute x9, waiting for transfers between devices: 7.26 us -> 8.56 us  [the longest x1 3.61 us: four_way_tail(): came_far = lax.ppermute(send, 'tensor', chip_swap)]
  transfers between devices with their start and end apart: 9 -> 9, of which waited for: 4 -> 4; matrix products, arithmetic and copies ran while one was open for 14% -> 3% of each run, Pallas kernels for 18% -> 20%
where the time goes in v2:
time: 76 us; the launch traced here: 75.3 us
  starting transfers between devices  26.2 us (34%)
  Pallas kernels  20.7 us (27%)
  local copies, waits for them, and re-layouts  15.6 us (21%)
  waiting for transfers between devices  8.56 us (11%)
  other arithmetic  3.49 us (5%)
  between operations  0.84 us (1%)
    pallas_call x13, Pallas kernels, run(): pl.pallas_call(kernel, out_shape=shapes[0] if single else shapes, in_spec...  20.7 us
    unnamed x21, local copies, waits for them, and re-layouts  15.3 us
    ppermute x3, starting transfers between devices, body(): keys.append(lax.ppermute(last, 'seq', up))  12.3 us
    ppermute x3, starting transfers between devices, body(): values.append(lax.ppermute(values[-1], 'seq', up))  12.2 us
    ppermute x1, waiting for transfers between devices, four_way_tail(): came_far = lax.ppermute(send, 'tensor', chip_swap)  3.61 us
    ppermute x1, waiting for transfers between devices, four_way_tail(): came = lax.ppermute(send, 'tensor', core_swap)  1.86 us
    ppermute x1, waiting for transfers between devices, four_way_tail(): came_near = lax.ppermute(send_near, 'tensor', core_swap)  1.85 us
    ppermute x1, starting transfers between devices, four_way_tail(): came_far = lax.ppermute(send, 'tensor', chip_swap)  1.54 us
  transfers between devices with their start and end apart: 9, of which 4 were waited for; matrix products, arithmetic and copies ran while one was open for 3% of the time, Pallas kernels for 20%

profile of v2, /device:TPU:0, one launch (start us, length us, event | category | flops | bytes accessed | tf_op | source)
XLA Modules:
  0.0 75.3 jit_solution(6903342549129268712)
XLA Ops:
  1.2 0.9 %copy-done.8 = bf16[256,512]{1,0:T(8,128)(2,1)S(1)} copy-done((bf16[256,512]{1,0:T(8,128)(2,1)S(1)}, bf16[256,512]{1,0:T(8,128)(2,1)}, u32[]{:S(2)}) %copy-start.8) | copy-done | bytes 262168
  2.3 5.7 %collective-permute-start = (bf16[256,512]{1,0:T(8,128)(2,1)S(1)}, bf16[256,512]{1,0:T(8,128)(2,1)}, u32[]{:S(2)}, u32[]{:S(2)}) collective-permute-start(bf16[256,512]{1,0:T(8,128)(2,1)S(1)} %rotate_keys.1.refs_2_), channel_id=1, source_target_pairs={{0,4},{4,8},{8,12},{1,5},{5,9},{9,13},{2,6},{6,10},{10,14},{3,7},{... | collective-permute-start | bytes 786440 | tf_op jit(solution)/shard_map/ppermute | solution.py:319
  8.0 3.5 %collective-permute-start.2 = (bf16[256,512]{1,0:T(8,128)(2,1)}, bf16[256,512]{1,0:T(8,128)(2,1)}, u32[]{:S(2)}, u32[]{:S(2)}) collective-permute-start(bf16[256,512]{1,0:T(8,128)(2,1)} %refs_3_.1), channel_id=1, source_target_pairs={{0,4},{4,8},{8,12},{1,5},{5,9},{9,13},{2,6},{6,10},{10,14},{3,7},{... | collective-permute-start | bytes 786440 | tf_op jit(solution)/shard_map/ppermute | solution.py:317
  11.5 1.0 %copy-done.5 = bf16[256,1024]{1,0:T(8,128)(2,1)S(1)} copy-done((bf16[256,1024]{1,0:T(8,128)(2,1)S(1)}, bf16[256,1024]{1,0:T(8,128)(2,1)}, u32[]{:S(2)}) %copy-start.5) | copy-done | bytes 524312
  14.6 3.8 %collective-permute-start.1 = (bf16[256,512]{1,0:T(8,128)(2,1)}, bf16[256,512]{1,0:T(8,128)(2,1)S(1)}, u32[]{:S(2)}, u32[]{:S(2)}) collective-permute-start(bf16[256,512]{1,0:T(8,128)(2,1)} %collective-permute-done.refs_2_), channel_id=1, source_target_pairs={{0,4},{4,8},{8,12},{1,5},{5,9},{9,13},{2,6},{6,10},{10,14},{3,7},{... | collective-permute-start | bytes 786440 | tf_op jit(solution)/shard_map/ppermute | solution.py:319
  18.4 1.2 %collective-permute-done.2.refs_3_ = bf16[256,512]{1,0:T(8,128)(2,1)} collective-permute-done((bf16[256,512]{1,0:T(8,128)(2,1)}, bf16[256,512]{1,0:T(8,128)(2,1)}, u32[]{:S(2)}, u32[]{:S(2)}) %collective-permute-start.2) | collective-permute-done | bytes 262176 | tf_op jit(solution)/shard_map/ppermute | solution.py:317
  19.7 5.1 %collective-permute-start.4 = (bf16[256,512]{1,0:T(8,128)(2,1)}, bf16[256,512]{1,0:T(8,128)(2,1)}, u32[]{:S(2)}, u32[]{:S(2)}) collective-permute-start(bf16[256,512]{1,0:T(8,128)(2,1)} %collective-permute-done.2.refs_3_), channel_id=1, source_target_pairs={{0,4},{4,8},{8,12},{1,5},{5,9},{9,13},{2,6},{6,10},{10,14},{3,7},{... | collective-permute-start | bytes 786440 | tf_op jit(solution)/shard_map/ppermute | solution.py:317
  24.7 1.4 %multiply_reduce_fusion = f32[]{:T(128)} fusion(f32[3840]{0:T(1024)} %param.12), kind=kLoop, calls=%fused_computation.2 | loop fusion | flops 7679 | bytes 15364 | tf_op jit(solution)/shard_map/reduce_sum | solution.py:222
  26.8 4.3 %attend_1.1 = (f32[2,512,256]{2,1,0:T(8,128)S(1)}, f32[2,512,128]{2,1,0:T(8,128)S(1)}) custom-call(s32[1]{0:T(128)} %bitcast.4.refs_0_, bf16[256,1024]{1,0:T(8,128)(2,1)S(1)} %rotate_queries.1.refs_1_, bf16[256,512]{1,0:T(8,128)(2,1)} %collective-permute-done.refs_2_, bf16[256,512]{1,0:T(8,128)(2,1)} %collective-permute-done.2.refs_3_, ...), custom_call_target="tpu_custom_call" | custom-call | tf_op jit(solution)/shard_map/attend_1/pallas_call | solution.py:23
  31.9 2.8 %collective-permute-start.3 = (bf16[256,512]{1,0:T(8,128)(2,1)S(1)}, bf16[256,512]{1,0:T(8,128)(2,1)S(1)}, u32[]{:S(2)}, u32[]{:S(2)}) collective-permute-start(bf16[256,512]{1,0:T(8,128)(2,1)S(1)} %collective-permute-done.1.refs_2_), channel_id=1, source_target_pairs={{0,4},{4,8},{8,12},{1,5},{5,9},{9,13},{2,6},{6,10},{10,14},{3,7},{... | collective-permute-start | bytes 786440 | tf_op jit(solution)/shard_map/ppermute | solution.py:319
  34.7 3.7 %collective-permute-start.5 = (bf16[256,512]{1,0:T(8,128)(2,1)}, bf16[256,512]{1,0:T(8,128)(2,1)S(1)}, u32[]{:S(2)}, u32[]{:S(2)}) collective-permute-start(bf16[256,512]{1,0:T(8,128)(2,1)} %collective-permute-done.4.refs_3_), channel_id=1, source_target_pairs={{0,4},{4,8},{8,12},{1,5},{5,9},{9,13},{2,6},{6,10},{10,14},{3,7},{... | collective-permute-start | bytes 786440 | tf_op jit(solution)/shard_map/ppermute | solution.py:317
  39.2 1.0 %copy-done.3 = bf16[256,960]{0,1:T(8,128)(2,1)S(1)} copy-done((bf16[256,960]{0,1:T(8,128)(2,1)S(1)}, bf16[256,960]{0,1:T(8,128)(2,1)}, u32[]{:S(2)}) %copy-start.3) | copy-done | bytes 491544
  40.5 3.2 %copy-done = bf16[1024,3840]{1,0:T(8,128)(2,1)S(1)} copy-done((bf16[1024,3840]{1,0:T(8,128)(2,1)S(1)}, bf16[1024,3840]{1,0:T(8,128)(2,1)}, u32[]{:S(2)}) %copy-start) | copy-done | bytes 7864344
  43.7 2.1 %direction.1.refs_3_ = bf16[8,1024]{1,0:T(8,128)(2,1)S(1)} custom-call(f32[1,3840]{1,0:T(1,128)S(1)} %reshape.23.unit_ref, bf16[1024,3840]{1,0:T(8,128)(2,1)S(1)} %copy-done), custom_call_target="tpu_custom_call" | custom-call | tf_op jit(solution)/shard_map/direction/pallas_call | solution.py:23
  45.9 4.2 %attend_2.1 = (f32[2,512,256]{2,1,0:T(8,128)S(1)}, f32[2,512,128]{2,1,0:T(8,128)S(1)}) custom-call(s32[1]{0:T(128)} %bitcast.4.refs_0_, bf16[256,1024]{1,0:T(8,128)(2,1)S(1)} %rotate_queries.1.refs_1_, bf16[256,512]{1,0:T(8,128)(2,1)S(1)} %collective-permute-done.1.refs_2_, bf16[256,512]{1,0:T(8,128)(2,1)} %collective-permute-done.4.refs_3_, ...), custom_call_target="tpu_custom_call" | custom-call | tf_op jit(solution)/shard_map/attend_2/pallas_call | solution.py:23
  50.1 3.3 %attend_3.1.refs_1_ = bf16[256,1024]{1,0:T(8,128)(2,1)S(1)} custom-call(s32[1]{0:T(128)} %bitcast.4.refs_0_, bf16[256,1024]{1,0:T(8,128)(2,1)S(1)} %rotate_queries.1.refs_1_, bf16[256,512]{1,0:T(8,128)(2,1)S(1)} %collective-permute-done.3.refs_2_, bf16[256,512]{1,0:T(8,128)(2,1)S(1)} %collective-permute-done.5.refs_3_, ...), custom_call_target="tpu_custom_call" | custom-call | tf_op jit(solution)/shard_map/attend_3/pallas_call | solution.py:23
  53.4 3.2 %copy-done.1 = bf16[1024,3840]{1,0:T(8,128)(2,1)S(1)} copy-done((bf16[1024,3840]{1,0:T(8,128)(2,1)S(1)}, bf16[1024,3840]{1,0:T(8,128)(2,1)}, u32[]{:S(2)}) %copy-start.1) | copy-done | bytes 7864344
  56.7 2.1 %project_far.1 = (bf16[976,256]{1,0:T(8,128)(2,1)S(1)}, f32[960,256]{1,0:T(8,128)S(1)}, f32[1,256]{1,0:T(1,128)S(1)}) custom-call(s32[3]{0:T(128)S(1)} %add_add_fusion.1.refs_0_, bf16[256,1024]{1,0:T(8,128)(2,1)S(1)} %attend_3.1.refs_1_, bf16[1024,3840]{1,0:T(8,128)(2,1)S(1)} %copy-done.1, bf16[8,1024]{1,0:T(8,128)(2,1)S(1)} %direction.1.refs_3_, ...), custom_call_target="tpu_custom_call" | custom-call | tf_op jit(solution)/shard_map/project_far/pallas_call | solution.py:23
  58.8 1.9 %collective-permute-done.6.came_ref = bf16[976,256]{1,0:T(8,128)(2,1)S(1)} collective-permute-done((bf16[976,256]{1,0:T(8,128)(2,1)S(1)}, bf16[976,256]{1,0:T(8,128)(2,1)S(1)}, u32[]{:S(2)}, u32[]{:S(2)}) %collective-permute-start.6) | collective-permute-done | bytes 499744 | tf_op jit(solution)/shard_map/ppermute | solution.py:247
  60.8 1.5 %collective-permute-start.8 = (bf16[976,256]{1,0:T(8,128)(2,1)S(1)}, bf16[976,256]{1,0:T(8,128)(2,1)S(1)}, u32[]{:S(2)}, u32[]{:S(2)}) collective-permute-start(bf16[976,256]{1,0:T(8,128)(2,1)S(1)} %get-tuple-element.41), channel_id=1, source_target_pairs={{0,2},{2,0},{1,3},{3,1},{4,6},{6,4},{5,7},{7,5},{8,10},{10,8},{9,1... | collective-permute-start | bytes 1499144 | tf_op jit(solution)/shard_map/ppermute | solution.py:255
  62.4 3.2 %copy-done.2 = bf16[1024,3840]{1,0:T(8,128)(2,1)S(1)} copy-done((bf16[1024,3840]{1,0:T(8,128)(2,1)S(1)}, bf16[1024,3840]{1,0:T(8,128)(2,1)}, u32[]{:S(2)}) %copy-start.2) | copy-done | bytes 7864344
  65.6 2.8 %project_near.1 = (bf16[960,256]{1,0:T(8,128)(2,1)}, f32[960,256]{1,0:T(8,128)S(1)}) custom-call(s32[3]{0:T(128)S(1)} %add_add_fusion.refs_0_, bf16[256,1024]{1,0:T(8,128)(2,1)S(1)} %attend_3.1.refs_1_, bf16[1024,3840]{1,0:T(8,128)(2,1)S(1)} %copy-done.2), custom_call_target="tpu_custom_call" | custom-call | tf_op jit(solution)/shard_map/project_near/pallas_call | solution.py:23
  68.7 1.9 %collective-permute-done.7.came_ref = bf16[960,256]{1,0:T(8,128)(2,1)S(1)} collective-permute-done((bf16[960,256]{1,0:T(8,128)(2,1)}, bf16[960,256]{1,0:T(8,128)(2,1)S(1)}, u32[]{:S(2)}, u32[]{:S(2)}) %collective-permute-start.7) | collective-permute-done | bytes 491552 | tf_op jit(solution)/shard_map/ppermute | solution.py:264
  70.7 3.6 %collective-permute-done.8.came_ref = bf16[976,256]{1,0:T(8,128)(2,1)S(1)} collective-permute-done((bf16[976,256]{1,0:T(8,128)(2,1)S(1)}, bf16[976,256]{1,0:T(8,128)(2,1)S(1)}, u32[]{:S(2)}, u32[]{:S(2)}) %collective-permute-start.8) | collective-permute-done | bytes 499744 | tf_op jit(solution)/shard_map/ppermute | solution.py:255
  (38 shorter events, 6.9 us)
Async XLA Ops:
  1.2 1.0 %copy-start.8 = (bf16[256,512]{1,0:T(8,128)(2,1)S(1)}, bf16[256,512]{1,0:T(8,128)(2,1)}, u32[]{:S(2)}) copy-start(bf16[256,512]{1,0:T(8,128)(2,1)} %ref.3) | copy-start | bytes 786436
  2.3 12.3 %collective-permute-start = (bf16[256,512]{1,0:T(8,128)(2,1)S(1)}, bf16[256,512]{1,0:T(8,128)(2,1)}, u32[]{:S(2)}, u32[]{:S(2)}) collective-permute-start(bf16[256,512]{1,0:T(8,128)(2,1)S(1)} %rotate_keys.1.refs_2_), channel_id=1, source_target_pairs={{0,4},{4,8},{8,12},{1,5},{5,9},{9,13},{2,6},{6,10},{10,14},{3,7},{... | collective-permute-start | bytes 786440 | tf_op jit(solution)/shard_map/ppermute | solution.py:319
  8.0 11.7 %collective-permute-start.2 = (bf16[256,512]{1,0:T(8,128)(2,1)}, bf16[256,512]{1,0:T(8,128)(2,1)}, u32[]{:S(2)}, u32[]{:S(2)}) collective-permute-start(bf16[256,512]{1,0:T(8,128)(2,1)} %refs_3_.1), channel_id=1, source_target_pairs={{0,4},{4,8},{8,12},{1,5},{5,9},{9,13},{2,6},{6,10},{10,14},{3,7},{... | collective-permute-start | bytes 786440 | tf_op jit(solution)/shard_map/ppermute | solution.py:317
  11.5 1.0 %copy-start.5 = (bf16[256,1024]{1,0:T(8,128)(2,1)S(1)}, bf16[256,1024]{1,0:T(8,128)(2,1)}, u32[]{:S(2)}) copy-start(bf16[256,1024]{1,0:T(8,128)(2,1)} %ref.2) | copy-start | bytes 1572868
  12.8 1.0 %copy-start.9 = (bf16[256,512]{1,0:T(8,128)(2,1)S(1)}, bf16[256,512]{1,0:T(8,128)(2,1)}, u32[]{:S(2)}) copy-start(bf16[256,512]{1,0:T(8,128)(2,1)} %refs_3_.1) | copy-start | bytes 786436
  14.6 17.3 %collective-permute-start.1 = (bf16[256,512]{1,0:T(8,128)(2,1)}, bf16[256,512]{1,0:T(8,128)(2,1)S(1)}, u32[]{:S(2)}, u32[]{:S(2)}) collective-permute-start(bf16[256,512]{1,0:T(8,128)(2,1)} %collective-permute-done.refs_2_), channel_id=1, source_target_pairs={{0,4},{4,8},{8,12},{1,5},{5,9},{9,13},{2,6},{6,10},{10,14},{3,7},{... | collective-permute-start | bytes 786440 | tf_op jit(solution)/shard_map/ppermute | solution.py:319
  19.7 15.1 %collective-permute-start.4 = (bf16[256,512]{1,0:T(8,128)(2,1)}, bf16[256,512]{1,0:T(8,128)(2,1)}, u32[]{:S(2)}, u32[]{:S(2)}) collective-permute-start(bf16[256,512]{1,0:T(8,128)(2,1)} %collective-permute-done.2.refs_3_), channel_id=1, source_target_pairs={{0,4},{4,8},{8,12},{1,5},{5,9},{9,13},{2,6},{6,10},{10,14},{3,7},{... | collective-permute-start | bytes 786440 | tf_op jit(solution)/shard_map/ppermute | solution.py:317
  31.1 0.8 %copy-start.6 = (f32[2,512,128]{2,1,0:T(8,128)}, f32[2,512,128]{2,1,0:T(8,128)S(1)}, u32[]{:S(2)}) copy-start(f32[2,512,128]{2,1,0:T(8,128)S(1)} %get-tuple-element.30.refs_5_) | copy-start | bytes 1572868
  31.9 18.2 %collective-permute-start.3 = (bf16[256,512]{1,0:T(8,128)(2,1)S(1)}, bf16[256,512]{1,0:T(8,128)(2,1)S(1)}, u32[]{:S(2)}, u32[]{:S(2)}) collective-permute-start(bf16[256,512]{1,0:T(8,128)(2,1)S(1)} %collective-permute-done.1.refs_2_), channel_id=1, source_target_pairs={{0,4},{4,8},{8,12},{1,5},{5,9},{9,13},{2,6},{6,10},{10,14},{3,7},{... | collective-permute-start | bytes 786440 | tf_op jit(solution)/shard_map/ppermute | solution.py:319
  34.7 15.4 %collective-permute-start.5 = (bf16[256,512]{1,0:T(8,128)(2,1)}, bf16[256,512]{1,0:T(8,128)(2,1)S(1)}, u32[]{:S(2)}, u32[]{:S(2)}) collective-permute-start(bf16[256,512]{1,0:T(8,128)(2,1)} %collective-permute-done.4.refs_3_), channel_id=1, source_target_pairs={{0,4},{4,8},{8,12},{1,5},{5,9},{9,13},{2,6},{6,10},{10,14},{3,7},{... | collective-permute-start | bytes 786440 | tf_op jit(solution)/shard_map/ppermute | solution.py:317
  39.2 1.0 %copy-start.3 = (bf16[256,960]{0,1:T(8,128)(2,1)S(1)}, bf16[256,960]{0,1:T(8,128)(2,1)}, u32[]{:S(2)}) copy-start(bf16[256,960]{0,1:T(8,128)(2,1)} %param.11) | copy-start | bytes 1474564
  40.4 3.3 %copy-start = (bf16[1024,3840]{1,0:T(8,128)(2,1)S(1)}, bf16[1024,3840]{1,0:T(8,128)(2,1)}, u32[]{:S(2)}) copy-start(bf16[1024,3840]{1,0:T(8,128)(2,1)} %refs_2_.3) | copy-start | bytes 23592964
  43.7 2.2 %copy-start.7 = (f32[2,512,128]{2,1,0:T(8,128)S(1)}, f32[2,512,128]{2,1,0:T(8,128)}, u32[]{:S(2)}) copy-start(f32[2,512,128]{2,1,0:T(8,128)} %copy-done.6) | copy-start | bytes 1572868
  53.4 3.2 %copy-start.1 = (bf16[1024,3840]{1,0:T(8,128)(2,1)S(1)}, bf16[1024,3840]{1,0:T(8,128)(2,1)}, u32[]{:S(2)}) copy-start(bf16[1024,3840]{1,0:T(8,128)(2,1)} %refs_2_.3) | copy-start | bytes 23592964
  56.7 13.9 %copy-start.4 = (bf16[256,960]{0,1:T(8,128)(2,1)S(1)}, bf16[256,960]{0,1:T(8,128)(2,1)}, u32[]{:S(2)}) copy-start(bf16[256,960]{0,1:T(8,128)(2,1)} %param.11) | copy-start | bytes 1474564
  58.7 1.9 %collective-permute-start.6 = (bf16[976,256]{1,0:T(8,128)(2,1)S(1)}, bf16[976,256]{1,0:T(8,128)(2,1)S(1)}, u32[]{:S(2)}, u32[]{:S(2)}) collective-permute-start(bf16[976,256]{1,0:T(8,128)(2,1)S(1)} %get-tuple-element.40), channel_id=1, source_target_pairs={{0,1},{1,0},{2,3},{3,2},{4,5},{5,4},{6,7},{7,6},{8,9},{9,8},{10,11... | collective-permute-start | bytes 1499144 | tf_op jit(solution)/shard_map/ppermute | solution.py:247
  60.8 13.5 %collective-permute-start.8 = (bf16[976,256]{1,0:T(8,128)(2,1)S(1)}, bf16[976,256]{1,0:T(8,128)(2,1)S(1)}, u32[]{:S(2)}, u32[]{:S(2)}) collective-permute-start(bf16[976,256]{1,0:T(8,128)(2,1)S(1)} %get-tuple-element.41), channel_id=1, source_target_pairs={{0,2},{2,0},{1,3},{3,1},{4,6},{6,4},{5,7},{7,5},{8,10},{10,8},{9,1... | collective-permute-start | bytes 1499144 | tf_op jit(solution)/shard_map/ppermute | solution.py:255
  62.4 3.2 %copy-start.2 = (bf16[1024,3840]{1,0:T(8,128)(2,1)S(1)}, bf16[1024,3840]{1,0:T(8,128)(2,1)}, u32[]{:S(2)}) copy-start(bf16[1024,3840]{1,0:T(8,128)(2,1)} %refs_2_.3) | copy-start | bytes 23592964
  68.5 2.1 %collective-permute-start.7 = (bf16[960,256]{1,0:T(8,128)(2,1)}, bf16[960,256]{1,0:T(8,128)(2,1)S(1)}, u32[]{:S(2)}, u32[]{:S(2)}) collective-permute-start(bf16[960,256]{1,0:T(8,128)(2,1)} %get-tuple-element.44), channel_id=1, source_target_pairs={{0,1},{1,0},{2,3},{3,2},{4,5},{5,4},{6,7},{7,6},{8,9},{9,8},{10,11... | collective-permute-start | bytes 1474568 | tf_op jit(solution)/shard_map/ppermute | solution.py:264
